TPU v7x, 512 devices: a whole 4x4x16 slice. The times are simulated.
512 devices in a mesh: wide: 64 (over x, z_lo, core), narrow: 8 (over z_hi, y).
Axes of the slice: x: 4, y: 4, z: 16 (z_hi: 2, z_lo: 8; z = z_hi * 8 + z_lo), core: 2. Of those that a mesh axis runs over, the one named last changes fastest.
Arguments:
- vectors: float32 [4096, 65536], P('narrow', 'wide'), may hold values from -6 to 6
- weights: bfloat16 [5, 256, 256, 512], P(None, 'wide', 'narrow'), may hold values from -0.25 to 0.25
Outputs:
- transformed: float32 [4096, 65536], P('narrow', 'wide')
All inputs are finite; a program needn't handle non-finite values.
Results may differ from a plain program's by a relative error of at most 0.0003.
Values may be sent and summed in bfloat16 or wider, within the bound.
No kernel may reach another device: no remote copies, remote signals or barrier semaphores. Data moves between devices by JAX's collectives and lax.ppermute only.
A program may use at most 64 MiB of HBM per device.

v0:
```python
import jax
import jax.numpy as jnp
from jax import lax
from jax.sharding import Mesh
from jax.sharding import PartitionSpec as P

NARROW = ("narrow_0", "narrow_1")


def swapped(shard, axis, apart):
    return lax.ppermute(shard, axis, [(i, i ^ 1 << apart) for i in range(lax.axis_size(axis))])


def joined_along(blocks, dim):
    shape = list(blocks.shape[1:])
    shape[dim] *= blocks.shape[0]
    return jnp.moveaxis(blocks, 0, dim).reshape(shape)


def stacked_from(shard, axes, sequence):
    blocks = shard
    for k in sequence:
        blocks = lax.all_gather(blocks, axes[k])
    done = sequence[::-1]
    back = [done.index(k) for k in range(len(axes))]
    blocks = blocks.transpose(*back, *range(len(axes), blocks.ndim))
    return blocks.reshape(-1, *shard.shape)


def gathered_by_axis(shard, axes, sequence, dim):
    return joined_along(stacked_from(shard, axes, sequence), dim)


def pair_local(current, level_bit):
    columns, block_count, block_size = current.shape
    stride = 1 << level_bit
    grouped = current.reshape(columns, block_count // (2 * stride), 2, stride, block_size)
    paired = jnp.concatenate([grouped[:, :, 0], grouped[:, :, 1]], -1)
    spread = jnp.broadcast_to(
        paired[:, :, None], (columns, block_count // (2 * stride), 2, stride, 2 * block_size)
    )
    return spread.reshape(columns, block_count, 2 * block_size)


def upper_side(level_bit):
    return lax.axis_index("wide") // (1 << level_bit) % 2


def pair_wide(current, level_bit):
    partner = swapped(current, "wide", level_bit)
    upper_bit = upper_side(level_bit)
    lower_half = jnp.where(upper_bit == 1, partner, current)
    upper_half = jnp.where(upper_bit == 1, current, partner)
    return jnp.concatenate([lower_half, upper_half], -1)


def contract(paired, matrix_rows):
    return jnp.einsum(
        "cbi,boi->cbo", paired, matrix_rows.astype(jnp.float32), precision=lax.Precision.HIGHEST
    )


def on_device(vectors, weights):
    columns, coeffs = vectors.shape
    block_size = weights.shape[3] // 2
    current = vectors.reshape(columns, coeffs // block_size, block_size)
    wide_top = lax.axis_size("wide").bit_length() - 1
    wide_bits = [0, wide_top // 2, wide_top - 1]
    gathered = gathered_by_axis(weights, NARROW, (0, 1), 2)
    for level_index in range(5):
        if level_index < 2:
            paired = pair_local(current, level_index)
            current = contract(paired, gathered[level_index])
        else:
            paired = pair_wide(current, wide_bits[level_index - 2])
            current = contract(paired, gathered[level_index])
    return current.reshape(columns, coeffs)


def solution(mesh):
    torus = Mesh(mesh.devices.reshape(mesh.shape["wide"], 2, 4), ("wide", "narrow_0", "narrow_1"))
    in_specs = (P(NARROW, "wide"), P(None, "wide", NARROW, None))
    out_specs = P(NARROW, "wide")
    return jax.shard_map(
        on_device, mesh=torus, in_specs=in_specs, out_specs=out_specs, check_vma=False
    )
```

profile of v0, /device:TPU:480, one launch (start us, length us, event | category | flops | bytes accessed | tf_op | source)
XLA Modules:
  0.0 434.6 jit_solution(1789773096415021390)
XLA Ops:
  6.5 0.7 all-gather.5.cloned.1.call-update
  7.3 0.0 all-gather.7.cloned.1.call-start
  7.3 81.2 %all-gather.5.cloned.1.call-done = bf16[10,4,32,512]{3,2,1,0:T(8,128)(2,1)} async-done(((bf16[5,4,32,512]{3,2,1,0:T(8,128)(2,1)}), bf16[10,4,32,512]{3,2,1,0:T(8,128)(2,1)}) %all-gather.5.cloned.1.call-update) | async-done | bytes 1310736 | tf_op jit(solution)/shard_map/all_gather | solution.py:23
  88.5 3.0 reshape_reshape.3
  91.5 1.1 slice_bitcast_fusion.2
  92.6 0.7 slice_bitcast_fusion.3
  93.3 1.8 pad_maximum_fusion
  95.2 0.4 copy.24
  95.6 57.8 %all-gather.7.cloned.1.call-done = bf16[8,5,4,32,512]{4,3,2,1,0:T(8,128)(2,1)} async-done(((bf16[2,5,4,32,512]{4,3,2,1,0:T(8,128)(2,1)}), bf16[8,5,4,32,512]{4,3,2,1,0:T(8,128)(2,1)}) %all-gather.7.cloned.1.call-update) | async-done | bytes 5242896 | tf_op jit(solution)/shard_map/all_gather | solution.py:23
  153.4 2.9 copy.13
  156.3 1.8 fusion.21
  158.1 0.6 broadcast_in_dim.21
  158.7 2.3 fusion.22
  161.0 0.2 slice_bitcast_fusion.1
  161.2 1.5 maximum_bitcast_fusion
  162.7 1.9 copy.14
  164.6 0.6 broadcast_in_dim.24
  165.2 0.6 copy-done.2
  165.8 2.3 convolution_bitcast_fusion
  168.1 2.1 collective-permute-start
  170.3 4.1 collective-permute-done
  174.3 2.1 broadcast_select_fusion.1
  176.4 2.2 fusion.15
  178.6 6.9 %collective-permute-start.1 = (f32[512,4,256]{0,2,1:T(8,128)S(1)}, f32[512,4,256]{0,2,1:T(8,128)}, u32[]{:S(2)}, u32[]{:S(2)}) collective-permute-start(f32[512,4,256]{0,2,1:T(8,128)S(1)} %fusion.15), channel_id=1, source_target_pairs={{0,64},{8,72},{16,80},{24,88},{32,96},{40,104},{48,112},{56,120},{... | collective-permute-start | bytes 6291464 | tf_op jit(solution)/shard_map/ppermute | solution.py:11
  185.6 181.4 %collective-permute-done.1 = f32[512,4,256]{0,2,1:T(8,128)} collective-permute-done((f32[512,4,256]{0,2,1:T(8,128)S(1)}, f32[512,4,256]{0,2,1:T(8,128)}, u32[]{:S(2)}, u32[]{:S(2)}) %collective-permute-start.1) | collective-permute-done | bytes 2097184 | tf_op jit(solution)/shard_map/ppermute | solution.py:11
  367.0 2.1 broadcast_select_fusion.3
  369.1 2.2 fusion.12
  371.3 4.9 %collective-permute-start.2 = (f32[512,4,256]{0,2,1:T(8,128)S(1)}, f32[512,4,256]{0,2,1:T(8,128)}, u32[]{:S(2)}, u32[]{:S(2)}) collective-permute-start(f32[512,4,256]{0,2,1:T(8,128)S(1)} %fusion.12), channel_id=1, source_target_pairs={{0,256},{8,264},{16,272},{24,280},{32,288},{40,296},{48,304},{56,3... | collective-permute-start | bytes 6291464 | tf_op jit(solution)/shard_map/ppermute | solution.py:11
  376.2 45.4 %collective-permute-done.2 = f32[512,4,256]{0,2,1:T(8,128)} collective-permute-done((f32[512,4,256]{0,2,1:T(8,128)S(1)}, f32[512,4,256]{0,2,1:T(8,128)}, u32[]{:S(2)}, u32[]{:S(2)}) %collective-permute-start.2) | collective-permute-done | bytes 2097184 | tf_op jit(solution)/shard_map/ppermute | solution.py:11
  421.6 2.1 broadcast_select_fusion.5
  423.7 2.2 fusion.8
  425.9 1.8 copy.18
  (7 shorter events, 0.0 us)
Async XLA Ops:
  6.5 81.9 %all-gather.5.cloned.1.call-start = ((), (), s32[]{:S(2)}) async-start(), calls=%async_computation | async-start | bytes 1966080 | tf_op jit(solution)/shard_map/all_gather | solution.py:23
  7.3 146.1 %all-gather.7.cloned.1.call-start = ((), (), s32[]{:S(2)}) async-start(), calls=%async_computation.1 | async-start | bytes 6553600 | tf_op jit(solution)/shard_map/all_gather | solution.py:23
  164.6 1.2 copy-start.2
  168.1 6.2 %collective-permute-start = (f32[512,4,256]{0,2,1:T(8,128)S(1)}, f32[512,4,256]{0,2,1:T(8,128)}, u32[]{:S(2)}, u32[]{:S(2)}) collective-permute-start(f32[512,4,256]{0,2,1:T(8,128)S(1)} %convolution_bitcast_fusion), channel_id=1, source_target_pairs={{0,8},{8,0},{16,24},{24,16},{32,40},{40,32},{48,56},{56,48},{64,72... | collective-permute-start | bytes 6291464 | tf_op jit(solution)/shard_map/ppermute | solution.py:11
  170.3 6.2 %copy-start.1 = (bf16[1,4,8,32,512]{4,3,2,1,0:T(8,128)(2,1)S(1)}, bf16[1,4,8,32,512]{4,3,2,1,0:T(8,128)(2,1)}, u32[]{:S(2)}) copy-start(bf16[1,4,8,32,512]{4,3,2,1,0:T(8,128)(2,1)} %get-tuple-element.8) | copy-start | bytes 3145732
  178.6 188.4 %collective-permute-start.1 = (f32[512,4,256]{0,2,1:T(8,128)S(1)}, f32[512,4,256]{0,2,1:T(8,128)}, u32[]{:S(2)}, u32[]{:S(2)}) collective-permute-start(f32[512,4,256]{0,2,1:T(8,128)S(1)} %fusion.15), channel_id=1, source_target_pairs={{0,64},{8,72},{16,80},{24,88},{32,96},{40,104},{48,112},{56,120},{... | collective-permute-start | bytes 6291464 | tf_op jit(solution)/shard_map/ppermute | solution.py:11
  185.6 183.6 %copy-start = (bf16[1,4,8,32,512]{4,3,2,1,0:T(8,128)(2,1)S(1)}, bf16[1,4,8,32,512]{4,3,2,1,0:T(8,128)(2,1)}, u32[]{:S(2)}) copy-start(bf16[1,4,8,32,512]{4,3,2,1,0:T(8,128)(2,1)} %get-tuple-element.7) | copy-start | bytes 3145732
  371.3 50.4 %collective-permute-start.2 = (f32[512,4,256]{0,2,1:T(8,128)S(1)}, f32[512,4,256]{0,2,1:T(8,128)}, u32[]{:S(2)}, u32[]{:S(2)}) collective-permute-start(f32[512,4,256]{0,2,1:T(8,128)S(1)} %fusion.12), channel_id=1, source_target_pairs={{0,256},{8,264},{16,272},{24,280},{32,288},{40,296},{48,304},{56,3... | collective-permute-start | bytes 6291464 | tf_op jit(solution)/shard_map/ppermute | solution.py:11
Sparse Core Ops, SparseCore 0:
  9.4 78.9 all-gather.4
  90.6 62.7 all-gather.6
where the time goes:
time: 441 us; the launch traced here: 435 us
  waiting for transfers between devices  371 us (84%)
  local copies, waits for them, and re-layouts  15.7 us (4%)
  starting transfers between devices  13.9 us (3%)
  between operations  13.7 us (3%)
  matrix products  11.1 us (3%)
  other arithmetic  9.56 us (2%)
    ppermute x3, waiting for transfers between devices, swapped(): lax.ppermute(shard, axis, [(i, i ^ 1 << apart) for i in range(lax.axis_si...  231 us
    all_gather x2, waiting for transfers between devices, stacked_from(): blocks = lax.all_gather(blocks, axes[k])  139 us
    ppermute x3, starting transfers between devices, swapped(): lax.ppermute(shard, axis, [(i, i ^ 1 << apart) for i in range(lax.axis_si...  13.9 us
    dot_general x5, matrix products, contract(): jnp.einsum('cbi,boi->cbo', paired, matrix_rows.astype(jnp.float32), preci...  11.1 us
  transfers between devices with their start and end apart: 5, of which 5 were waited for; matrix products, arithmetic and copies ran while one was open for 2% of the time, Pallas kernels for 0%

commit v1 on v0

v1 whole, which is shorter than its diff:
```python
import functools

import jax
import jax.numpy as jnp
from jax import lax
from jax.experimental import pallas as pl
from jax.experimental.pallas import tpu as pltpu
from jax.sharding import Mesh
from jax.sharding import PartitionSpec as P

NARROW = ("narrow_0", "narrow_1")
FLOOR = 2.0 ** -3.875
SPAN = 2.0 ** 3.875 - 2.0 ** -3.875
LANES = 128
SCALE_ROWS = 16


def swapped(shard, axis, apart):
    return lax.ppermute(shard, axis, [(i, i ^ 1 << apart) for i in range(lax.axis_size(axis))])


def assemble(matrix, own_ref, other_ref, half):
    parts, _, blocks, rows, _ = own_ref.shape
    for part in range(parts):
        for block in range(blocks):
            for ref, side in ((own_ref, half), (other_ref, 1 - half)):
                start = pl.multiple_of(side * (parts * rows) + part * rows, rows)
                matrix[block, pl.ds(start, rows), :] = ref[part, 0, block]


def split(x):
    high = x.astype(jnp.bfloat16)
    return high, (x - high.astype(jnp.float32)).astype(jnp.bfloat16)


def product(parts, matrix):
    dims = (((1,), (1,)), ((), ()))
    dots = [lax.dot_general(part, matrix, dims, preferred_element_type=jnp.float32) for part in parts]
    return dots[0] + dots[1]


def encode(value, out_ref):
    rows, columns = value.shape
    top = jnp.max(jnp.abs(value), axis=1, keepdims=True)
    top = jnp.maximum(jnp.broadcast_to(top, (rows, LANES)) * 1.01, 1e-30).astype(jnp.bfloat16)
    top = top.astype(jnp.float32)
    out_ref[pl.ds(rows * (columns // LANES), SCALE_ROWS), :] = top.T[:SCALE_ROWS].astype(jnp.bfloat16)
    gain = SPAN / top
    for tile in range(columns // LANES):
        x = value[:, tile * LANES:(tile + 1) * LANES]
        t = jnp.abs(x) * gain + FLOOR
        for _ in range(5):
            t = t * t
        out_ref[pl.ds(tile * rows, rows), :] = jnp.where(x < 0, -t, t).astype(jnp.bfloat16)


def decode(code_ref, rows, columns):
    tiles = columns // LANES
    top = code_ref[pl.ds(rows * tiles, SCALE_ROWS), :].astype(jnp.float32)
    gain = jnp.broadcast_to(top[:1], (LANES, LANES)).T[:rows] * (1.0 / SPAN)
    values = []
    for tile in range(tiles):
        g = code_ref[pl.ds(tile * rows, rows), :].astype(jnp.float32)
        t = jnp.exp(jnp.log(jnp.abs(g)) * (1.0 / 32.0))
        y = (t - FLOOR) * gain
        values.append(jnp.where(g < 0, -y, y))
    return jnp.concatenate(values, axis=1)


def blocks_of(value, count, size):
    return [split(value[:, k * size:(k + 1) * size]) for k in range(count)]


def local_body(bits_ref, x_ref, own0, other0, own1, other1, out_ref, matrix0, matrix1):
    @pl.when(pl.program_id(0) == 0)
    def _():
        assemble(matrix0, own0, other0, bits_ref[0])
        assemble(matrix1, own1, other1, bits_ref[0])

    count, size = matrix0.shape[:2]
    value = x_ref[...]
    for level, matrix in enumerate((matrix0, matrix1)):
        parts = blocks_of(value, count, size)
        outs = []
        for k in range(count):
            low, high = parts[k & ~(1 << level)], parts[k | 1 << level]
            outs.append(product(low, matrix[k, :, :size]) + product(high, matrix[k, :, size:]))
        value = jnp.concatenate(outs, axis=1)
    out_ref[...] = value


def cross_level(mine, partner, matrix, upper, count, size):
    own_parts, partner_parts = blocks_of(mine, count, size), blocks_of(partner, count, size)
    own_at = pl.multiple_of(upper * size, size)
    partner_at = pl.multiple_of((1 - upper) * size, size)
    outs = []
    for k in range(count):
        outs.append(
            product(own_parts[k], matrix[k, :, pl.ds(own_at, size)])
            + product(partner_parts[k], matrix[k, :, pl.ds(partner_at, size)])
        )
    return jnp.concatenate(outs, axis=1)


def core_body(bits_ref, mine_ref, partner_ref, own, other, out_ref, code_ref, matrix):
    assemble(matrix, own, other, bits_ref[0])
    count, size = matrix.shape[:2]
    value = cross_level(mine_ref[...], partner_ref[...], matrix, bits_ref[1], count, size)
    out_ref[...] = value
    encode(value, code_ref)


def middle_body(bits_ref, mine_ref, partner_ref, own, other, out_ref, code_ref, matrix):
    assemble(matrix, own, other, bits_ref[0])
    count, size = matrix.shape[:2]
    partner = decode(partner_ref, *mine_ref.shape)
    value = cross_level(mine_ref[...], partner, matrix, bits_ref[2], count, size)
    out_ref[...] = value
    encode(value, code_ref)


def last_body(bits_ref, mine_ref, partner_ref, own, other, *rest):
    out_ref, matrix = rest[-2:]
    assemble(matrix, own, other, bits_ref[0])
    count, size = matrix.shape[:2]
    partner = decode(partner_ref, *mine_ref.shape)
    out_ref[...] = cross_level(mine_ref[...], partner, matrix, bits_ref[3], count, size)


def on_device(vectors, weights, chunks=4):
    columns, coeffs = vectors.shape
    _, count, share, width = weights.shape
    size = width // 2
    parts = lax.axis_size("narrow_1")
    rows = columns // chunks
    code_rows = rows * (coeffs // LANES) + SCALE_ROWS
    wide_top = lax.axis_size("wide").bit_length() - 1
    wide_bits = [0, wide_top // 2, wide_top - 1]
    place = lax.axis_index("wide")
    bits = jnp.stack([lax.axis_index("narrow_0")] + [place >> bit & 1 for bit in wide_bits])

    first, second = weights[:3], weights[3:]
    own_first = lax.all_gather(first, "narrow_1")
    other_shard = swapped(first, "narrow_0", 0)
    other_first = lax.all_gather(other_shard, "narrow_1")
    second_later, _ = lax.optimization_barrier((second, other_shard))
    own_second = lax.all_gather(second, "narrow_1")
    other_second = lax.all_gather(swapped(second_later, "narrow_0", 0), "narrow_1")

    def matrix_spec(level):
        return pl.BlockSpec((parts, 1, count, share, width), lambda i, bits: (0, level, 0, 0, 0))

    matrix_scratch = pltpu.VMEM((count, size, width), jnp.bfloat16)

    def cost(rows_done, levels, bytes_accessed):
        return pl.CostEstimate(
            flops=4 * levels * rows_done * coeffs * width, bytes_accessed=bytes_accessed, transcendentals=0
        )

    matrix_bytes = 2 * count * size * width

    def call(body, grid, in_specs, out_specs, out_shape, scratch, estimate, aliases={}):
        return pl.pallas_call(
            body,
            grid_spec=pltpu.PrefetchScalarGridSpec(
                num_scalar_prefetch=1, grid=grid, in_specs=in_specs, out_specs=out_specs, scratch_shapes=scratch
            ),
            out_shape=out_shape,
            input_output_aliases=aliases,
            cost_estimate=estimate,
            compiler_params=pltpu.CompilerParams(vmem_limit_bytes=48 << 20),
        )

    def row_spec(index):
        return pl.BlockSpec((rows, coeffs), lambda i, bits: (index, 0))

    moving = pl.BlockSpec((rows, coeffs), lambda i, bits: (i, 0))
    whole = pl.BlockSpec((rows, coeffs), lambda i, bits: (0, 0))
    code_spec = pl.BlockSpec((code_rows, LANES), lambda i, bits: (0, 0))
    code_shape = jax.ShapeDtypeStruct((code_rows, LANES), jnp.bfloat16)
    chunk_shape = jax.ShapeDtypeStruct((rows, coeffs), jnp.float32)

    current = call(
        local_body, (chunks,), [moving] + [matrix_spec(level) for level in (0, 0, 1, 1)], moving,
        jax.ShapeDtypeStruct((columns, coeffs), jnp.float32), [matrix_scratch] * 2,
        cost(columns, 2, 8 * columns * coeffs + 2 * matrix_bytes),
    )(bits, vectors, own_first, other_first, own_first, other_first)
    partner = swapped(current, "wide", wide_bits[0])

    pieces = []
    for c in range(chunks):
        mine, code = call(
            core_body, (1,), [row_spec(c), row_spec(c), matrix_spec(2), matrix_spec(2)], [whole, code_spec],
            [chunk_shape, code_shape], [matrix_scratch], cost(rows, 1, 14 * rows * coeffs + matrix_bytes),
        )(bits, current, partner, own_first, other_first)
        pieces.append((mine, swapped(code, "wide", wide_bits[1])))
    later = []
    for mine, code in pieces:
        mine, code = call(
            middle_body, (1,), [whole, code_spec, matrix_spec(0), matrix_spec(0)], [whole, code_spec],
            [chunk_shape, code_shape], [matrix_scratch], cost(rows, 1, 12 * rows * coeffs + matrix_bytes),
        )(bits, mine, code, own_second, other_second)
        later.append((mine, swapped(code, "wide", wide_bits[2])))
    out = None
    for c, (mine, code) in enumerate(later):
        operands = [bits, mine, code, own_second, other_second]
        specs = [whole, code_spec, matrix_spec(1), matrix_spec(1)]
        if out is not None:
            operands.append(out)
            specs.append(pl.BlockSpec(memory_space=pl.ANY))
        out = call(
            last_body, (1,), specs, row_spec(c), jax.ShapeDtypeStruct((columns, coeffs), jnp.float32),
            [matrix_scratch], cost(rows, 1, 10 * rows * coeffs + matrix_bytes),
            {} if out is None else {5: 0},
        )(*operands)
    return out


def solution(mesh):
    names = ("wide", "narrow_0", "narrow_1")
    torus = Mesh(mesh.devices.reshape(mesh.shape["wide"], 2, mesh.shape["narrow"] // 2), names)
    in_specs = (P(NARROW, "wide"), P(None, "wide", NARROW, None))
    out_specs = P(NARROW, "wide")
    return jax.shard_map(
        on_device, mesh=torus, in_specs=in_specs, out_specs=out_specs, check_vma=False
    )
```

time: 441 us -> 274 us (0.62)
  the two profiles are of different devices: /device:TPU:480 before, /device:TPU:2 now
where the time goes in v1:
time: 274 us
  waiting for transfers between devices  133 us (49%)
  starting transfers between devices  71.3 us (26%)
  Pallas kernels  41.2 us (15%)
  local copies, waits for them, and re-layouts  14.7 us (5%)
  between operations  13.4 us (5%)
    ppermute x11, waiting for transfers between devices, swapped(): lax.ppermute(shard, axis, [(i, i ^ 1 << apart) for i in range(lax.axis_si...  78.8 us
    ppermute x11, starting transfers between devices, swapped(): lax.ppermute(shard, axis, [(i, i ^ 1 << apart) for i in range(lax.axis_si...  71.2 us
    all_gather x1, waiting for transfers between devices, on_device(): other_first = lax.all_gather(other_shard, 'narrow_1')  46.4 us
    pallas_call x4, Pallas kernels, on_device(): call(core_body, (1,), [row_spec(c), row_spec(c), matrix_spec(2), matrix_s...  14.4 us
    unnamed x34, local copies, waits for them, and re-layouts  11.3 us
    pallas_call x4, Pallas kernels, on_device(): call(last_body, (1,), specs, row_spec(c), jax.ShapeDtypeStruct((columns,...  9.12 us
    pallas_call x4, Pallas kernels, on_device(): call(middle_body, (1,), [whole, code_spec, matrix_spec(0), matrix_spec(0)...  8.92 us
    pallas_call x1, Pallas kernels, on_device(): call(local_body, (chunks,), [moving] + [matrix_spec(level) for level in (...  8.82 us
  transfers between devices with their start and end apart: 15, of which 5 were waited for; matrix products, arithmetic and copies ran while one was open for 1% of the time, Pallas kernels for 14%

profile of v1, /device:TPU:2, one launch (start us, length us, event | category | flops | bytes accessed | tf_op | source)
XLA Modules:
  0.0 273.6 jit_solution(13533699021237431456)
XLA Ops:
  6.5 1.8 slice.6
  8.4 15.7 %collective-permute-start = (bf16[3,4,32,512]{3,2,1,0:T(8,128)(2,1)}, bf16[3,4,32,512]{3,2,1,0:T(8,128)(2,1)S(1)}, u32[]{:S(2)}, u32[]{:S(2)}) collective-permute-start(bf16[3,4,32,512]{3,2,1,0:T(8,128)(2,1)} %slice.6), channel_id=1, source_target_pairs={{0,4},{4,0},{1,5},{5,1},{2,6},{6,2},{3,7},{7,3},{8,12},{12,8},{9,1... | collective-permute-start | bytes 1179656 | tf_op jit(solution)/shard_map/ppermute | solution.py:19
  24.1 13.9 %collective-permute-done = bf16[3,4,32,512]{3,2,1,0:T(8,128)(2,1)S(1)} collective-permute-done((bf16[3,4,32,512]{3,2,1,0:T(8,128)(2,1)}, bf16[3,4,32,512]{3,2,1,0:T(8,128)(2,1)S(1)}, u32[]{:S(2)}, u32[]{:S(2)}) %collective-permute-start) | collective-permute-done | bytes 393248 | tf_op jit(solution)/shard_map/ppermute | solution.py:19
  38.8 1.7 slice.7
  40.6 7.5 %all-gather.9.cloned.1.call-done = bf16[12,4,32,512]{3,2,1,0:T(8,128)(2,1)} async-done(((bf16[3,4,32,512]{3,2,1,0:T(8,128)(2,1)}), bf16[12,4,32,512]{3,2,1,0:T(8,128)(2,1)}) %all-gather.9.cloned.1.call-update) | async-done | bytes 1572880 | tf_op jit(solution)/shard_map/all_gather | solution.py:143
  48.2 46.4 %all-gather.11.cloned.1.call-done = bf16[12,4,32,512]{3,2,1,0:T(8,128)(2,1)} async-done(((bf16[3,4,32,512]{3,2,1,0:T(8,128)(2,1)}), bf16[12,4,32,512]{3,2,1,0:T(8,128)(2,1)}) %all-gather.11.cloned.1.call-update) | async-done | bytes 1572880 | tf_op jit(solution)/shard_map/all_gather | solution.py:145
  94.6 1.4 copy-done.3
  97.4 8.8 %shard_map.28.mine_ref = f32[512,1024]{1,0:T(8,128)} custom-call(s32[4]{0:T(128)S(1)} %pad_add_fusion.bits_ref, f32[512,1024]{1,0:T(8,128)} %x_ref.1, bf16[4,3,4,32,512]{4,3,2,1,0:T(8,128)(2,1)S(1)} %bitcast.24, bf16[4,3,4,32,512]{4,3,2,1,0:T(8,128)(2,1)S(1)} %bitcast.30, bf16[4,3,4,32,512]{4,3,2,1,0:T(8,128)(2,1)S(1)} %bitcast.25, ...), custom_call_target="tpu_custom_call" | custom-call | flops 2147483648 | bytes 6291456 | tf_op jit(solution)/shard_map/pallas_call | solution.py:183
  106.2 1.9 collective-permute-start.1
  108.1 12.9 %collective-permute-start.3 = (bf16[2,4,32,512]{3,2,1,0:T(8,128)(2,1)S(1)}, bf16[2,4,32,512]{3,2,1,0:T(8,128)(2,1)}, u32[]{:S(2)}, u32[]{:S(2)}) collective-permute-start(bf16[2,4,32,512]{3,2,1,0:T(8,128)(2,1)S(1)} %copy-done.15), channel_id=1, source_target_pairs={{0,4},{4,0},{1,5},{5,1},{2,6},{6,2},{3,7},{7,3},{8,12},{12,8},{9,1... | collective-permute-start | bytes 786440 | tf_op jit(solution)/shard_map/ppermute | solution.py:19
  121.0 13.8 %collective-permute-done.3 = bf16[2,4,32,512]{3,2,1,0:T(8,128)(2,1)} collective-permute-done((bf16[2,4,32,512]{3,2,1,0:T(8,128)(2,1)S(1)}, bf16[2,4,32,512]{3,2,1,0:T(8,128)(2,1)}, u32[]{:S(2)}, u32[]{:S(2)}) %collective-permute-start.3) | collective-permute-done | bytes 262176 | tf_op jit(solution)/shard_map/ppermute | solution.py:19
  134.9 3.6 %shard_map.35 = (f32[128,1024]{1,0:T(8,128)S(1)}, bf16[1040,128]{1,0:T(8,128)(2,1)}) custom-call(s32[4]{0:T(128)S(1)} %pad_add_fusion.bits_ref, f32[512,1024]{1,0:T(8,128)} %shard_map.28.mine_ref, f32[512,1024]{1,0:T(8,128)} %collective-permute-done.1.partner_ref, bf16[4,3,4,32,512]{4,3,2,1,0:T(8,128)(2,1)S(1)} %bitcast.26, ...), custom_call_target="tpu_custom_call" | custom-call | flops 268435456 | bytes 2883584 | tf_op jit(solution)/shard_map/pallas_call | solution.py:192
  139.3 14.0 %collective-permute-start.9 = (bf16[1040,128]{1,0:T(8,128)(2,1)}, bf16[1040,128]{1,0:T(8,128)(2,1)}, u32[]{:S(2)}, u32[]{:S(2)}) collective-permute-start(bf16[1040,128]{1,0:T(8,128)(2,1)} %get-tuple-element.36), channel_id=1, source_target_pairs={{0,64},{8,72},{16,80},{24,88},{32,96},{40,104},{48,112},{56,120},{... | collective-permute-start | bytes 798728 | tf_op jit(solution)/shard_map/ppermute | solution.py:19
  153.2 3.6 %shard_map.33 = (f32[128,1024]{1,0:T(8,128)S(1)}, bf16[1040,128]{1,0:T(8,128)(2,1)}) custom-call(s32[4]{0:T(128)S(1)} %pad_add_fusion.bits_ref, f32[512,1024]{1,0:T(8,128)} %shard_map.28.mine_ref, f32[512,1024]{1,0:T(8,128)} %collective-permute-done.1.partner_ref, bf16[4,3,4,32,512]{4,3,2,1,0:T(8,128)(2,1)S(1)} %bitcast.27, ...), custom_call_target="tpu_custom_call" | custom-call | flops 268435456 | bytes 2883584 | tf_op jit(solution)/shard_map/pallas_call | solution.py:192
  157.6 1.9 collective-permute-start.7
  159.5 3.6 %shard_map.31 = (f32[128,1024]{1,0:T(8,128)S(1)}, bf16[1040,128]{1,0:T(8,128)(2,1)}) custom-call(s32[4]{0:T(128)S(1)} %pad_add_fusion.bits_ref, f32[512,1024]{1,0:T(8,128)} %shard_map.28.mine_ref, f32[512,1024]{1,0:T(8,128)} %collective-permute-done.1.partner_ref, bf16[4,3,4,32,512]{4,3,2,1,0:T(8,128)(2,1)S(1)} %bitcast.28, ...), custom_call_target="tpu_custom_call" | custom-call | flops 268435456 | bytes 2883584 | tf_op jit(solution)/shard_map/pallas_call | solution.py:192
  163.9 7.8 %collective-permute-start.5 = (bf16[1040,128]{1,0:T(8,128)(2,1)}, bf16[1040,128]{1,0:T(8,128)(2,1)S(1)}, u32[]{:S(2)}, u32[]{:S(2)}) collective-permute-start(bf16[1040,128]{1,0:T(8,128)(2,1)} %get-tuple-element.28), channel_id=1, source_target_pairs={{0,64},{8,72},{16,80},{24,88},{32,96},{40,104},{48,112},{56,120},{... | collective-permute-start | bytes 798728 | tf_op jit(solution)/shard_map/ppermute | solution.py:19
  171.8 3.6 %shard_map.29 = (f32[128,1024]{1,0:T(8,128)S(1)}, bf16[1040,128]{1,0:T(8,128)(2,1)}) custom-call(s32[4]{0:T(128)S(1)} %pad_add_fusion.bits_ref, f32[512,1024]{1,0:T(8,128)} %shard_map.28.mine_ref, f32[512,1024]{1,0:T(8,128)} %collective-permute-done.1.partner_ref, bf16[4,3,4,32,512]{4,3,2,1,0:T(8,128)(2,1)S(1)} %bitcast.29, ...), custom_call_target="tpu_custom_call" | custom-call | flops 268435456 | bytes 2883584 | tf_op jit(solution)/shard_map/pallas_call | solution.py:192
  176.1 1.9 collective-permute-start.2
  178.1 51.1 %collective-permute-done.9.partner_ref = bf16[1040,128]{1,0:T(8,128)(2,1)} collective-permute-done((bf16[1040,128]{1,0:T(8,128)(2,1)}, bf16[1040,128]{1,0:T(8,128)(2,1)}, u32[]{:S(2)}, u32[]{:S(2)}) %collective-permute-start.9) | collective-permute-done | bytes 266272 | tf_op jit(solution)/shard_map/ppermute | solution.py:19
  232.7 2.7 shard_map.36
  235.4 4.1 %collective-permute-start.10 = (bf16[1040,128]{1,0:T(8,128)(2,1)S(1)}, bf16[1040,128]{1,0:T(8,128)(2,1)S(1)}, u32[]{:S(2)}, u32[]{:S(2)}) collective-permute-start(bf16[1040,128]{1,0:T(8,128)(2,1)S(1)} %get-tuple-element.38), channel_id=1, source_target_pairs={{0,256},{8,264},{16,272},{24,280},{32,288},{40,296},{48,304},{56,3... | collective-permute-start | bytes 798728 | tf_op jit(solution)/shard_map/ppermute | solution.py:19
  240.6 2.7 shard_map.34
  243.3 3.5 %collective-permute-start.8 = (bf16[1040,128]{1,0:T(8,128)(2,1)S(1)}, bf16[1040,128]{1,0:T(8,128)(2,1)S(1)}, u32[]{:S(2)}, u32[]{:S(2)}) collective-permute-start(bf16[1040,128]{1,0:T(8,128)(2,1)S(1)} %get-tuple-element.34), channel_id=1, source_target_pairs={{0,256},{8,264},{16,272},{24,280},{32,288},{40,296},{48,304},{56,3... | collective-permute-start | bytes 798728 | tf_op jit(solution)/shard_map/ppermute | solution.py:19
  246.8 1.8 shard_map.32
  248.6 4.0 %collective-permute-start.6 = (bf16[1040,128]{1,0:T(8,128)(2,1)S(1)}, bf16[1040,128]{1,0:T(8,128)(2,1)S(1)}, u32[]{:S(2)}, u32[]{:S(2)}) collective-permute-start(bf16[1040,128]{1,0:T(8,128)(2,1)S(1)} %get-tuple-element.30), channel_id=1, source_target_pairs={{0,256},{8,264},{16,272},{24,280},{32,288},{40,296},{48,304},{56,3... | collective-permute-start | bytes 798728 | tf_op jit(solution)/shard_map/ppermute | solution.py:19
  252.6 1.8 shard_map.30
  254.4 3.6 %collective-permute-start.4 = (bf16[1040,128]{1,0:T(8,128)(2,1)S(1)}, bf16[1040,128]{1,0:T(8,128)(2,1)S(1)}, u32[]{:S(2)}, u32[]{:S(2)}) collective-permute-start(bf16[1040,128]{1,0:T(8,128)(2,1)S(1)} %get-tuple-element.26), channel_id=1, source_target_pairs={{0,256},{8,264},{16,272},{24,280},{32,288},{40,296},{48,304},{56,3... | collective-permute-start | bytes 798728 | tf_op jit(solution)/shard_map/ppermute | solution.py:19
  258.0 2.3 shard_map.37.rest_0_
  260.2 2.3 shard_map.38.rest_0_
  262.5 2.3 shard_map.39.rest_0_
  264.8 2.3 shard_map.40
  (52 shorter events, 10.2 us)
Async XLA Ops:
  6.5 41.6 %all-gather.9.cloned.1.call-start = ((), (), s32[]{:S(2)}) async-start(), calls=%async_computation | async-start | bytes 1966080 | tf_op jit(solution)/shard_map/all_gather | solution.py:143
  8.3 86.2 %all-gather.11.cloned.1.call-start = ((), (), s32[]{:S(2)}) async-start(), calls=%async_computation.1 | async-start | bytes 1966080 | tf_op jit(solution)/shard_map/all_gather | solution.py:145
  8.4 29.6 %collective-permute-start = (bf16[3,4,32,512]{3,2,1,0:T(8,128)(2,1)}, bf16[3,4,32,512]{3,2,1,0:T(8,128)(2,1)S(1)}, u32[]{:S(2)}, u32[]{:S(2)}) collective-permute-start(bf16[3,4,32,512]{3,2,1,0:T(8,128)(2,1)} %slice.6), channel_id=1, source_target_pairs={{0,4},{4,0},{1,5},{5,1},{2,6},{6,2},{3,7},{7,3},{8,12},{12,8},{9,1... | collective-permute-start | bytes 1179656 | tf_op jit(solution)/shard_map/ppermute | solution.py:19
  38.0 0.7 copy-start.16
  38.7 139.3 %all-gather.13.cloned.1.call-start = ((), (), s32[]{:S(2)}) async-start(), calls=%async_computation.2 | async-start | bytes 1310720 | tf_op jit(solution)/shard_map/all_gather | solution.py:147
  40.5 137.6 %all-gather.15.cloned.1.call-start = ((), (), s32[]{:S(2)}) async-start(), calls=%async_computation.3 | async-start | bytes 1310720 | tf_op jit(solution)/shard_map/all_gather | solution.py:148
  94.6 1.4 copy-start.3
  96.0 1.4 copy-start.5
  97.4 10.8 %copy-start.15 = (bf16[2,4,32,512]{3,2,1,0:T(8,128)(2,1)S(1)}, bf16[2,4,32,512]{3,2,1,0:T(8,128)(2,1)}, u32[]{:S(2)}) copy-start(bf16[2,4,32,512]{3,2,1,0:T(8,128)(2,1)} %slice.7) | copy-start | bytes 786436
  97.4 37.5 %copy-start.4 = (bf16[12,4,32,512]{3,2,1,0:T(8,128)(2,1)S(1)}, bf16[12,4,32,512]{3,2,1,0:T(8,128)(2,1)}, u32[]{:S(2)}) copy-start(bf16[12,4,32,512]{3,2,1,0:T(8,128)(2,1)} %all-gather.9.cloned.1.call-done) | copy-start | bytes 4718596
  97.4 37.5 %copy-start.6 = (bf16[12,4,32,512]{3,2,1,0:T(8,128)(2,1)S(1)}, bf16[12,4,32,512]{3,2,1,0:T(8,128)(2,1)}, u32[]{:S(2)}) copy-start(bf16[12,4,32,512]{3,2,1,0:T(8,128)(2,1)} %all-gather.11.cloned.1.call-done) | copy-start | bytes 4718596
  106.2 28.6 %collective-permute-start.1 = (f32[512,1024]{1,0:T(8,128)}, f32[512,1024]{1,0:T(8,128)}, u32[]{:S(2)}, u32[]{:S(2)}) collective-permute-start(f32[512,1024]{1,0:T(8,128)} %shard_map.28.mine_ref), channel_id=1, source_target_pairs={{0,8},{8,0},{16,24},{24,16},{32,40},{40,32},{48,56},{56,48},{64,72... | collective-permute-start | bytes 6291464 | tf_op jit(solution)/shard_map/ppermute | solution.py:19
  108.1 26.7 %collective-permute-start.3 = (bf16[2,4,32,512]{3,2,1,0:T(8,128)(2,1)S(1)}, bf16[2,4,32,512]{3,2,1,0:T(8,128)(2,1)}, u32[]{:S(2)}, u32[]{:S(2)}) collective-permute-start(bf16[2,4,32,512]{3,2,1,0:T(8,128)(2,1)S(1)} %copy-done.15), channel_id=1, source_target_pairs={{0,4},{4,0},{1,5},{5,1},{2,6},{6,2},{3,7},{7,3},{8,12},{12,8},{9,1... | collective-permute-start | bytes 786440 | tf_op jit(solution)/shard_map/ppermute | solution.py:19
  138.5 0.8 copy-start.13
  139.3 90.0 %collective-permute-start.9 = (bf16[1040,128]{1,0:T(8,128)(2,1)}, bf16[1040,128]{1,0:T(8,128)(2,1)}, u32[]{:S(2)}, u32[]{:S(2)}) collective-permute-start(bf16[1040,128]{1,0:T(8,128)(2,1)} %get-tuple-element.36), channel_id=1, source_target_pairs={{0,64},{8,72},{16,80},{24,88},{32,96},{40,104},{48,112},{56,120},{... | collective-permute-start | bytes 798728 | tf_op jit(solution)/shard_map/ppermute | solution.py:19
  156.8 0.8 copy-start.11
  157.6 81.9 %collective-permute-start.7 = (bf16[1040,128]{1,0:T(8,128)(2,1)}, bf16[1040,128]{1,0:T(8,128)(2,1)}, u32[]{:S(2)}, u32[]{:S(2)}) collective-permute-start(bf16[1040,128]{1,0:T(8,128)(2,1)} %get-tuple-element.32), channel_id=1, source_target_pairs={{0,64},{8,72},{16,80},{24,88},{32,96},{40,104},{48,112},{56,120},{... | collective-permute-start | bytes 798728 | tf_op jit(solution)/shard_map/ppermute | solution.py:19
  163.1 0.8 copy-start.9
  163.9 82.9 %collective-permute-start.5 = (bf16[1040,128]{1,0:T(8,128)(2,1)}, bf16[1040,128]{1,0:T(8,128)(2,1)S(1)}, u32[]{:S(2)}, u32[]{:S(2)}) collective-permute-start(bf16[1040,128]{1,0:T(8,128)(2,1)} %get-tuple-element.28), channel_id=1, source_target_pairs={{0,64},{8,72},{16,80},{24,88},{32,96},{40,104},{48,112},{56,120},{... | collective-permute-start | bytes 798728 | tf_op jit(solution)/shard_map/ppermute | solution.py:19
  175.3 0.8 copy-start.7
  176.1 76.4 %collective-permute-start.2 = (bf16[1040,128]{1,0:T(8,128)(2,1)}, bf16[1040,128]{1,0:T(8,128)(2,1)S(1)}, u32[]{:S(2)}, u32[]{:S(2)}) collective-permute-start(bf16[1040,128]{1,0:T(8,128)(2,1)} %get-tuple-element.23), channel_id=1, source_target_pairs={{0,64},{8,72},{16,80},{24,88},{32,96},{40,104},{48,112},{56,120},{... | collective-permute-start | bytes 798728 | tf_op jit(solution)/shard_map/ppermute | solution.py:19
  229.2 1.2 copy-start
  230.4 1.2 copy-start.2
  231.7 1.0 copy-start.14
  235.4 11.4 %copy-start.10 = (f32[128,1024]{1,0:T(8,128)S(1)}, f32[128,1024]{1,0:T(8,128)}, u32[]{:S(2)}) copy-start(f32[128,1024]{1,0:T(8,128)} %copy-done.9) | copy-start | bytes 1572868
  235.4 22.5 %collective-permute-start.10 = (bf16[1040,128]{1,0:T(8,128)(2,1)S(1)}, bf16[1040,128]{1,0:T(8,128)(2,1)S(1)}, u32[]{:S(2)}, u32[]{:S(2)}) collective-permute-start(bf16[1040,128]{1,0:T(8,128)(2,1)S(1)} %get-tuple-element.38), channel_id=1, source_target_pairs={{0,256},{8,264},{16,272},{24,280},{32,288},{40,296},{48,304},{56,3... | collective-permute-start | bytes 798728 | tf_op jit(solution)/shard_map/ppermute | solution.py:19
  239.5 1.0 copy-start.12
  243.3 9.3 %copy-start.1 = (bf16[8,4,32,512]{3,2,1,0:T(8,128)(2,1)S(1)}, bf16[8,4,32,512]{3,2,1,0:T(8,128)(2,1)}, u32[]{:S(2)}) copy-start(bf16[8,4,32,512]{3,2,1,0:T(8,128)(2,1)} %all-gather.13.cloned.1.call-done) | copy-start | bytes 3145732
  243.3 9.3 %copy-start.8 = (f32[128,1024]{1,0:T(8,128)S(1)}, f32[128,1024]{1,0:T(8,128)}, u32[]{:S(2)}) copy-start(f32[128,1024]{1,0:T(8,128)} %copy-done.7) | copy-start | bytes 1572868
  243.3 16.9 %collective-permute-start.8 = (bf16[1040,128]{1,0:T(8,128)(2,1)S(1)}, bf16[1040,128]{1,0:T(8,128)(2,1)S(1)}, u32[]{:S(2)}, u32[]{:S(2)}) collective-permute-start(bf16[1040,128]{1,0:T(8,128)(2,1)S(1)} %get-tuple-element.34), channel_id=1, source_target_pairs={{0,256},{8,264},{16,272},{24,280},{32,288},{40,296},{48,304},{56,3... | collective-permute-start | bytes 798728 | tf_op jit(solution)/shard_map/ppermute | solution.py:19
  248.6 13.9 %collective-permute-start.6 = (bf16[1040,128]{1,0:T(8,128)(2,1)S(1)}, bf16[1040,128]{1,0:T(8,128)(2,1)S(1)}, u32[]{:S(2)}, u32[]{:S(2)}) collective-permute-start(bf16[1040,128]{1,0:T(8,128)(2,1)S(1)} %get-tuple-element.30), channel_id=1, source_target_pairs={{0,256},{8,264},{16,272},{24,280},{32,288},{40,296},{48,304},{56,3... | collective-permute-start | bytes 798728 | tf_op jit(solution)/shard_map/ppermute | solution.py:19
  254.4 10.4 %collective-permute-start.4 = (bf16[1040,128]{1,0:T(8,128)(2,1)S(1)}, bf16[1040,128]{1,0:T(8,128)(2,1)S(1)}, u32[]{:S(2)}, u32[]{:S(2)}) collective-permute-start(bf16[1040,128]{1,0:T(8,128)(2,1)S(1)} %get-tuple-element.26), channel_id=1, source_target_pairs={{0,256},{8,264},{16,272},{24,280},{32,288},{40,296},{48,304},{56,3... | collective-permute-start | bytes 798728 | tf_op jit(solution)/shard_map/ppermute | solution.py:19
Sparse Core Ops, SparseCore 0:
  9.5 38.6 all-gather.8
  50.3 44.2 all-gather.10
  96.7 31.7 all-gather.12
  135.0 38.0 all-gather.14

commit v2 on v1

v2 whole, which is shorter than its diff:
```python
import functools

import jax
import jax.numpy as jnp
from jax import lax
from jax.experimental import pallas as pl
from jax.experimental.pallas import tpu as pltpu
from jax.sharding import Mesh
from jax.sharding import PartitionSpec as P

NARROW = ("narrow_0", "narrow_1")
FLOOR = 2.0 ** -3.875
SPAN = 2.0 ** 3.875 - 2.0 ** -3.875
LANES = 128
SCALE_ROWS = 16


def swapped(shard, axis, apart):
    return lax.ppermute(shard, axis, [(i, i ^ 1 << apart) for i in range(lax.axis_size(axis))])


def assemble(matrix, level, own_ref, other_refs, half, part):
    parts, _, blocks, rows, _ = own_ref.shape
    for block in range(blocks):
        for k in range(parts):
            start = pl.multiple_of((half * parts + k) * rows, rows)
            matrix[level, block, pl.ds(start, rows), :] = own_ref[k, level, block]
            place = (1 - half) * parts + ((part + (parts - k)) & (parts - 1))
            start = pl.multiple_of(place * rows, rows)
            matrix[level, block, pl.ds(start, rows), :] = other_refs[k][level, block]


def split(x):
    high = x.astype(jnp.bfloat16)
    return jnp.concatenate([high, (x - high.astype(jnp.float32)).astype(jnp.bfloat16)], axis=0)


def product(parts, matrix):
    dims = (((1,), (1,)), ((), ()))
    dots = lax.dot_general(parts, matrix, dims, preferred_element_type=jnp.float32)
    rows = parts.shape[0] // 2
    return dots[:rows] + dots[rows:]


def encode(value, out_ref):
    rows, columns = value.shape
    top = jnp.max(jnp.abs(value), axis=1, keepdims=True)
    top = jnp.maximum(jnp.broadcast_to(top, (rows, LANES)) * 1.01, 1e-30).astype(jnp.bfloat16)
    top = top.astype(jnp.float32)
    square = jnp.concatenate([top] * (LANES // rows), axis=0)
    out_ref[pl.ds(rows * (columns // LANES), SCALE_ROWS), :] = square.T[:SCALE_ROWS].astype(jnp.bfloat16)
    gain = SPAN / top
    for tile in range(columns // LANES):
        x = value[:, tile * LANES:(tile + 1) * LANES]
        t = jnp.abs(x) * gain + FLOOR
        for _ in range(5):
            t = t * t
        out_ref[pl.ds(tile * rows, rows), :] = jnp.where(x < 0, -t, t).astype(jnp.bfloat16)


def decode(code_ref, rows, columns):
    tiles = columns // LANES
    top = code_ref[pl.ds(rows * tiles, SCALE_ROWS), :].astype(jnp.float32)
    gain = jnp.broadcast_to(top[:1], (LANES, LANES)).T[:rows] * (1.0 / SPAN)
    values = []
    for tile in range(tiles):
        g = code_ref[pl.ds(tile * rows, rows), :].astype(jnp.float32)
        t = jnp.exp(jnp.log(jnp.abs(g)) * (1.0 / 32.0))
        y = (t - FLOOR) * gain
        values.append(jnp.where(g < 0, -y, y))
    return jnp.concatenate(values, axis=1)


def blocks_of(value, count, size):
    return [split(value[:, k * size:(k + 1) * size]) for k in range(count)]


def local_body(bits_ref, x_ref, own, *rest):
    others, out_ref, matrix = rest[:-2], rest[-2], rest[-1]
    levels, count, size = matrix.shape[:3]
    value = x_ref[...]
    for level in range(levels):
        assemble(matrix, level, own, others, bits_ref[0], bits_ref[1])
        parts = blocks_of(value, count, size)
        outs = []
        for k in range(count):
            low, high = parts[k & ~(1 << level)], parts[k | 1 << level]
            outs.append(
                product(low, matrix[level, k, :, :size]) + product(high, matrix[level, k, :, size:])
            )
        value = jnp.concatenate(outs, axis=1)
    out_ref[...] = value


def prepare_body(bits_ref, own, *rest):
    assemble(rest[-1], 0, own, rest[:-1], bits_ref[0], bits_ref[1])


def cross_level(mine, partner, matrix, upper):
    _, count, size, _ = matrix.shape
    own_parts, partner_parts = blocks_of(mine, count, size), blocks_of(partner, count, size)
    own_at = pl.multiple_of(upper * size, size)
    partner_at = pl.multiple_of((1 - upper) * size, size)
    outs = []
    for k in range(count):
        outs.append(
            product(own_parts[k], matrix[0, k, :, pl.ds(own_at, size)])
            + product(partner_parts[k], matrix[0, k, :, pl.ds(partner_at, size)])
        )
    return jnp.concatenate(outs, axis=1)


def core_body(bits_ref, mine_ref, partner_ref, matrix, out_ref, code_ref):
    value = cross_level(mine_ref[...], partner_ref[...], matrix, bits_ref[2])
    out_ref[...] = value
    encode(value, code_ref)


def middle_body(bits_ref, mine_ref, partner_ref, matrix, out_ref, code_ref):
    value = cross_level(mine_ref[...], decode(partner_ref, *mine_ref.shape), matrix, bits_ref[3])
    out_ref[...] = value
    encode(value, code_ref)


def last_body(bits_ref, mine_ref, partner_ref, matrix, *rest):
    rest[-1][...] = cross_level(mine_ref[...], decode(partner_ref, *mine_ref.shape), matrix, bits_ref[4])


def on_device(vectors, weights, chunks=8, window=2):
    columns, coeffs = vectors.shape
    _, count, share, width = weights.shape
    parts = lax.axis_size("narrow_1")
    rows = columns // chunks
    code_rows = rows * (coeffs // LANES) + SCALE_ROWS
    wide_top = lax.axis_size("wide").bit_length() - 1
    wide_bits = [0, wide_top // 2, wide_top - 1]
    place = lax.axis_index("wide")
    bits = jnp.stack(
        [lax.axis_index("narrow_0"), lax.axis_index("narrow_1")] + [place >> bit & 1 for bit in wide_bits]
    )

    def around(shard):
        return [shard] + [
            lax.ppermute(shard, "narrow_1", [(i, (i + k) % parts) for i in range(parts)]) for k in range(1, parts)
        ]

    own_early = lax.all_gather(weights[:3], "narrow_1")
    own_late = lax.all_gather(weights[3:], "narrow_1")
    first = swapped(weights[:2], "narrow_0", 0)
    turn, _ = lax.optimization_barrier((weights[2:4], first))
    second = swapped(turn, "narrow_0", 0)
    turn, _ = lax.optimization_barrier((weights[4:], second))
    third = swapped(turn, "narrow_0", 0)
    vectors, _ = lax.optimization_barrier((vectors, second))
    others = [around(first), around(second[:1]), around(second[1:]), around(third)]

    def call(body, in_specs, out_specs, out_shape, scratch, estimate, aliases={}):
        return pl.pallas_call(
            body,
            grid_spec=pltpu.PrefetchScalarGridSpec(
                num_scalar_prefetch=1, grid=(1,), in_specs=in_specs, out_specs=out_specs, scratch_shapes=scratch
            ),
            out_shape=out_shape,
            input_output_aliases=aliases,
            cost_estimate=estimate,
            compiler_params=pltpu.CompilerParams(vmem_limit_bytes=48 << 20),
        )

    def cost(rows_done, levels, bytes_accessed):
        return pl.CostEstimate(
            flops=4 * levels * rows_done * coeffs * width, bytes_accessed=bytes_accessed, transcendentals=0
        )

    size = width // 2
    matrix_bytes = 2 * count * size * width
    matrix_shape = (1, count, size, width)

    def gathered_spec(levels, at):
        return pl.BlockSpec((parts, levels, count, share, width), lambda i, bits: (0, at, 0, 0, 0))

    def shard_spec(levels, at):
        return pl.BlockSpec((levels, count, share, width), lambda i, bits: (at, 0, 0, 0))

    def prepared(own, own_at, other, other_at):
        return call(
            prepare_body, [gathered_spec(1, own_at)] + [shard_spec(1, other_at)] * parts,
            pl.BlockSpec(matrix_shape, lambda i, bits: (0, 0, 0, 0)),
            jax.ShapeDtypeStruct(matrix_shape, weights.dtype), [], cost(0, 0, 2 * matrix_bytes),
        )(bits, own, *other)

    def row_spec(index):
        return pl.BlockSpec((rows, coeffs), lambda i, bits: (index, 0))

    matrix_spec = pl.BlockSpec(matrix_shape, lambda i, bits: (0, 0, 0, 0))
    full = pl.BlockSpec((columns, coeffs), lambda i, bits: (0, 0))
    code_spec = pl.BlockSpec((code_rows, LANES), lambda i, bits: (0, 0))
    code_shape = jax.ShapeDtypeStruct((code_rows, LANES), jnp.bfloat16)
    chunk_shape = jax.ShapeDtypeStruct((rows, coeffs), jnp.float32)
    full_shape = jax.ShapeDtypeStruct((columns, coeffs), jnp.float32)

    current = call(
        local_body, [full, gathered_spec(2, 0)] + [shard_spec(2, 0)] * parts, full, full_shape,
        [pltpu.VMEM((2,) + matrix_shape[1:], weights.dtype)], cost(columns, 2, 8 * columns * coeffs + 2 * matrix_bytes),
    )(bits, vectors, own_early, *others[0])
    sent, _ = lax.optimization_barrier((current, others[1]))
    partner = swapped(sent, "wide", wide_bits[0])
    matrix = prepared(own_early, 2, others[1], 0)

    pieces = []
    for c in range(chunks):
        mine, code = call(
            core_body, [row_spec(c), row_spec(c), matrix_spec], [row_spec(0), code_spec],
            [chunk_shape, code_shape], [], cost(rows, 1, 14 * rows * coeffs + matrix_bytes),
        )(bits, current, partner, matrix)
        if c >= window:
            code, _ = lax.optimization_barrier((code, pieces[c - window][1]))
        pieces.append((mine, swapped(code, "wide", wide_bits[1])))
    matrix = prepared(own_late, 0, others[2], 0)
    later = []
    for mine, code in pieces:
        mine, code = call(
            middle_body, [row_spec(0), code_spec, matrix_spec], [row_spec(0), code_spec],
            [chunk_shape, code_shape], [], cost(rows, 1, 12 * rows * coeffs + matrix_bytes),
        )(bits, mine, code, matrix)
        later.append((mine, swapped(code, "wide", wide_bits[2])))
    matrix = prepared(own_late, 1, others[3], 0)
    out = None
    for c, (mine, code) in enumerate(later):
        operands = [bits, mine, code, matrix]
        specs = [row_spec(0), code_spec, matrix_spec]
        if out is not None:
            operands.append(out)
            specs.append(pl.BlockSpec(memory_space=pl.ANY))
        out = call(
            last_body, specs, row_spec(c), full_shape, [], cost(rows, 1, 10 * rows * coeffs + matrix_bytes),
            {} if out is None else {4: 0},
        )(*operands)
    return out


def solution(mesh):
    names = ("wide", "narrow_0", "narrow_1")
    torus = Mesh(mesh.devices.reshape(mesh.shape["wide"], 2, mesh.shape["narrow"] // 2), names)
    in_specs = (P(NARROW, "wide"), P(None, "wide", NARROW, None))
    out_specs = P(NARROW, "wide")
    return jax.shard_map(
        on_device, mesh=torus, in_specs=in_specs, out_specs=out_specs, check_vma=False
    )
```

time: 274 us -> 297 us (1.084)
  the two profiles are of different devices: /device:TPU:2 before, /device:TPU:480 now
where the time goes in v2:
time: 297 us; the launch traced here: 295 us
  starting transfers between devices  123 us (41%)
  waiting for transfers between devices  82.5 us (28%)
  Pallas kernels  51.8 us (17%)
  local copies, waits for them, and re-layouts  24.4 us (8%)
  between operations  14 us (5%)
    ppermute x20, waiting for transfers between devices, swapped(): lax.ppermute(shard, axis, [(i, i ^ 1 << apart) for i in range(lax.axis_si...  82.4 us
    ppermute x20, starting transfers between devices, swapped(): lax.ppermute(shard, axis, [(i, i ^ 1 << apart) for i in range(lax.axis_si...  81.2 us
    ppermute x12, starting transfers between devices, around(): lax.ppermute(shard, 'narrow_1', [(i, (i + k) % parts) for i in range(part...  41.3 us
    unnamed x64, local copies, waits for them, and re-layouts  19.7 us
    pallas_call x8, Pallas kernels, on_device(): call(core_body, [row_spec(c), row_spec(c), matrix_spec], [row_spec(0), co...  18.7 us
    pallas_call x8, Pallas kernels, on_device(): call(last_body, specs, row_spec(c), full_shape, [], cost(rows, 1, 10 * ro...  13.9 us
    pallas_call x8, Pallas kernels, on_device(): call(middle_body, [row_spec(0), code_spec, matrix_spec], [row_spec(0), co...  11.7 us
  transfers between devices with their start and end apart: 34, of which 5 were waited for; matrix products, arithmetic and copies ran while one was open for 1% of the time, Pallas kernels for 17%

profile of v2, /device:TPU:480, one launch (start us, length us, event | category | flops | bytes accessed | tf_op | source)
XLA Modules:
  0.0 295.3 jit_solution(3837924521376912691)
XLA Ops:
  10.3 6.3 %collective-permute-start = (bf16[2,4,32,512]{3,2,1,0:T(8,128)(2,1)S(1)}, bf16[2,4,32,512]{3,2,1,0:T(8,128)(2,1)S(1)}, u32[]{:S(2)}, u32[]{:S(2)}) collective-permute-start(bf16[2,4,32,512]{3,2,1,0:T(8,128)(2,1)S(1)} %get-tuple-element.90), channel_id=1, source_target_pairs={{0,4},{4,0},{1,5},{5,1},{2,6},{6,2},{3,7},{7,3},{8,12},{12,8},{9,1... | collective-permute-start | bytes 786440 | tf_op jit(solution)/shard_map/ppermute | solution.py:19
  16.6 23.8 %collective-permute-done.rest_0_ = bf16[2,4,32,512]{3,2,1,0:T(8,128)(2,1)S(1)} collective-permute-done((bf16[2,4,32,512]{3,2,1,0:T(8,128)(2,1)S(1)}, bf16[2,4,32,512]{3,2,1,0:T(8,128)(2,1)S(1)}, u32[]{:S(2)}, u32[]{:S(2)}) %collective-permute-start) | collective-permute-done | bytes 262176 | tf_op jit(solution)/shard_map/ppermute | solution.py:19
  42.7 3.5 %collective-permute-start.2 = (bf16[2,4,32,512]{3,2,1,0:T(8,128)(2,1)S(1)}, bf16[2,4,32,512]{3,2,1,0:T(8,128)(2,1)S(1)}, u32[]{:S(2)}, u32[]{:S(2)}) collective-permute-start(bf16[2,4,32,512]{3,2,1,0:T(8,128)(2,1)S(1)} %collective-permute-done.rest_0_), channel_id=1, source_target_pairs={{0,1},{1,2},{2,3},{3,0},{4,5},{5,6},{6,7},{7,4},{8,9},{9,10},{10,1... | collective-permute-start | bytes 786440 | tf_op jit(solution)/shard_map/ppermute | solution.py:144
  46.2 4.8 %collective-permute-start.3 = (bf16[2,4,32,512]{3,2,1,0:T(8,128)(2,1)S(1)}, bf16[2,4,32,512]{3,2,1,0:T(8,128)(2,1)S(1)}, u32[]{:S(2)}, u32[]{:S(2)}) collective-permute-start(bf16[2,4,32,512]{3,2,1,0:T(8,128)(2,1)S(1)} %collective-permute-done.rest_0_), channel_id=1, source_target_pairs={{0,2},{1,3},{2,0},{3,1},{4,6},{5,7},{6,4},{7,5},{8,10},{9,11},{10,... | collective-permute-start | bytes 786440 | tf_op jit(solution)/shard_map/ppermute | solution.py:144
  51.0 3.3 %collective-permute-start.4 = (bf16[2,4,32,512]{3,2,1,0:T(8,128)(2,1)S(1)}, bf16[2,4,32,512]{3,2,1,0:T(8,128)(2,1)S(1)}, u32[]{:S(2)}, u32[]{:S(2)}) collective-permute-start(bf16[2,4,32,512]{3,2,1,0:T(8,128)(2,1)S(1)} %collective-permute-done.rest_0_), channel_id=1, source_target_pairs={{0,3},{1,0},{2,1},{3,2},{4,7},{5,4},{6,5},{7,6},{8,11},{9,8},{10,9... | collective-permute-start | bytes 786440 | tf_op jit(solution)/shard_map/ppermute | solution.py:144
  54.4 18.3 %collective-permute-done.1 = bf16[2,4,32,512]{3,2,1,0:T(8,128)(2,1)S(1)} collective-permute-done((bf16[2,4,32,512]{3,2,1,0:T(8,128)(2,1)S(1)}, bf16[2,4,32,512]{3,2,1,0:T(8,128)(2,1)S(1)}, u32[]{:S(2)}, u32[]{:S(2)}) %collective-permute-start.1) | collective-permute-done | bytes 262176 | tf_op jit(solution)/shard_map/ppermute | solution.py:19
  72.7 3.5 %collective-permute-start.5 = (bf16[1,4,32,512]{3,2,1,0:T(8,128)(2,1)S(1)}, bf16[1,4,32,512]{3,2,1,0:T(8,128)(2,1)S(1)}, u32[]{:S(2)}, u32[]{:S(2)}) collective-permute-start(bf16[1,4,32,512]{3,2,1,0:T(8,128)(2,1)S(1)} %get-tuple-element.93.rest_0_), channel_id=1, source_target_pairs={{0,1},{1,2},{2,3},{3,0},{4,5},{5,6},{6,7},{7,4},{8,9},{9,10},{10,1... | collective-permute-start | bytes 393224 | tf_op jit(solution)/shard_map/ppermute | solution.py:144
  76.2 4.8 %collective-permute-start.6 = (bf16[1,4,32,512]{3,2,1,0:T(8,128)(2,1)S(1)}, bf16[1,4,32,512]{3,2,1,0:T(8,128)(2,1)S(1)}, u32[]{:S(2)}, u32[]{:S(2)}) collective-permute-start(bf16[1,4,32,512]{3,2,1,0:T(8,128)(2,1)S(1)} %get-tuple-element.93.rest_0_), channel_id=1, source_target_pairs={{0,2},{1,3},{2,0},{3,1},{4,6},{5,7},{6,4},{7,5},{8,10},{9,11},{10,... | collective-permute-start | bytes 393224 | tf_op jit(solution)/shard_map/ppermute | solution.py:144
  81.0 3.3 %collective-permute-start.7 = (bf16[1,4,32,512]{3,2,1,0:T(8,128)(2,1)S(1)}, bf16[1,4,32,512]{3,2,1,0:T(8,128)(2,1)S(1)}, u32[]{:S(2)}, u32[]{:S(2)}) collective-permute-start(bf16[1,4,32,512]{3,2,1,0:T(8,128)(2,1)S(1)} %get-tuple-element.93.rest_0_), channel_id=1, source_target_pairs={{0,3},{1,0},{2,1},{3,2},{4,7},{5,4},{6,5},{7,6},{8,11},{9,8},{10,9... | collective-permute-start | bytes 393224 | tf_op jit(solution)/shard_map/ppermute | solution.py:144
  87.4 4.6 %shard_map.28.mine_ref = f32[512,1024]{1,0:T(8,128)S(1)} custom-call(s32[5]{0:T(128)S(1)} %stack.23.bits_ref, f32[512,1024]{1,0:T(8,128)} %x_ref, bf16[4,3,4,32,512]{4,3,2,1,0:T(8,128)(2,1)S(1)} %bitcast.9, bf16[2,4,32,512]{3,2,1,0:T(8,128)(2,1)S(1)} %collective-permute-done.rest_0_, bf16[2,4,32,512]{3,2,1,0:T(8,128)(2,1)S(1)} %collective-permute-done.2.rest_1_, ...), custom_call_target="tpu_custom_call" | custom-call | flops 2147483648 | bytes 6291456 | tf_op jit(solution)/shard_map/pallas_call | solution.py:201
  106.4 7.8 %collective-permute-start.9 = (bf16[528,128]{1,0:T(8,128)(2,1)S(1)}, bf16[528,128]{1,0:T(8,128)(2,1)S(1)}, u32[]{:S(2)}, u32[]{:S(2)}) collective-permute-start(bf16[528,128]{1,0:T(8,128)(2,1)S(1)} %get-tuple-element.54), channel_id=1, source_target_pairs={{0,64},{8,72},{16,80},{24,88},{32,96},{40,104},{48,112},{56,120},{... | collective-permute-start | bytes 405512 | tf_op jit(solution)/shard_map/ppermute | solution.py:19
  120.0 33.4 %collective-permute-done.21.partner_ref = bf16[528,128]{1,0:T(8,128)(2,1)S(1)} collective-permute-done((bf16[528,128]{1,0:T(8,128)(2,1)S(1)}, bf16[528,128]{1,0:T(8,128)(2,1)S(1)}, u32[]{:S(2)}, u32[]{:S(2)}) %collective-permute-start.21) | collective-permute-done | bytes 135200 | tf_op jit(solution)/shard_map/ppermute | solution.py:19
  158.9 7.8 %collective-permute-start.10 = (bf16[528,128]{1,0:T(8,128)(2,1)S(1)}, bf16[528,128]{1,0:T(8,128)(2,1)S(1)}, u32[]{:S(2)}, u32[]{:S(2)}) collective-permute-start(bf16[528,128]{1,0:T(8,128)(2,1)S(1)} %get-tuple-element.55), channel_id=1, source_target_pairs={{0,64},{8,72},{16,80},{24,88},{32,96},{40,104},{48,112},{56,120},{... | collective-permute-start | bytes 405512 | tf_op jit(solution)/shard_map/ppermute | solution.py:19
  166.7 2.6 collective-permute-start.13
  169.3 2.7 collective-permute-start.14
  172.0 3.8 %collective-permute-start.15 = (bf16[1,4,32,512]{3,2,1,0:T(8,128)(2,1)S(1)}, bf16[1,4,32,512]{3,2,1,0:T(8,128)(2,1)S(1)}, u32[]{:S(2)}, u32[]{:S(2)}) collective-permute-start(bf16[1,4,32,512]{3,2,1,0:T(8,128)(2,1)S(1)} %get-tuple-element.92.rest_0_), channel_id=1, source_target_pairs={{0,3},{1,0},{2,1},{3,2},{4,7},{5,4},{6,5},{7,6},{8,11},{9,8},{10,9... | collective-permute-start | bytes 393224 | tf_op jit(solution)/shard_map/ppermute | solution.py:144
  175.8 6.4 %collective-permute-done.22.partner_ref = bf16[528,128]{1,0:T(8,128)(2,1)S(1)} collective-permute-done((bf16[528,128]{1,0:T(8,128)(2,1)S(1)}, bf16[528,128]{1,0:T(8,128)(2,1)S(1)}, u32[]{:S(2)}, u32[]{:S(2)}) %collective-permute-start.22) | collective-permute-done | bytes 135200 | tf_op jit(solution)/shard_map/ppermute | solution.py:19
  182.2 2.3 collective-permute-start.18
  184.6 2.8 shard_map.38
  190.1 2.8 shard_map.31
  193.6 7.8 %collective-permute-start.11 = (bf16[528,128]{1,0:T(8,128)(2,1)}, bf16[528,128]{1,0:T(8,128)(2,1)}, u32[]{:S(2)}, u32[]{:S(2)}) collective-permute-start(bf16[528,128]{1,0:T(8,128)(2,1)} %get-tuple-element.56), channel_id=1, source_target_pairs={{0,64},{8,72},{16,80},{24,88},{32,96},{40,104},{48,112},{56,120},{... | collective-permute-start | bytes 405512 | tf_op jit(solution)/shard_map/ppermute | solution.py:19
  202.1 4.0 %collective-permute-start.19 = (bf16[1,4,32,512]{3,2,1,0:T(8,128)(2,1)}, bf16[1,4,32,512]{3,2,1,0:T(8,128)(2,1)}, u32[]{:S(2)}, u32[]{:S(2)}) collective-permute-start(bf16[1,4,32,512]{3,2,1,0:T(8,128)(2,1)} %collective-permute-done.17.rest_0_), channel_id=1, source_target_pairs={{0,2},{1,3},{2,0},{3,1},{4,6},{5,7},{6,4},{7,5},{8,10},{9,11},{10,... | collective-permute-start | bytes 393224 | tf_op jit(solution)/shard_map/ppermute | solution.py:144
  206.7 2.8 collective-permute-start.20
  216.3 4.9 %collective-permute-start.30 = (bf16[528,128]{1,0:T(8,128)(2,1)S(1)}, bf16[528,128]{1,0:T(8,128)(2,1)S(1)}, u32[]{:S(2)}, u32[]{:S(2)}) collective-permute-start(bf16[528,128]{1,0:T(8,128)(2,1)S(1)} %get-tuple-element.85), channel_id=1, source_target_pairs={{0,256},{8,264},{16,272},{24,280},{32,288},{40,296},{48,304},{56,3... | collective-permute-start | bytes 405512 | tf_op jit(solution)/shard_map/ppermute | solution.py:19
  224.3 2.4 collective-permute-start.31
  233.2 8.0 %collective-permute-start.12 = (bf16[528,128]{1,0:T(8,128)(2,1)S(1)}, bf16[528,128]{1,0:T(8,128)(2,1)S(1)}, u32[]{:S(2)}, u32[]{:S(2)}) collective-permute-start(bf16[528,128]{1,0:T(8,128)(2,1)S(1)} %get-tuple-element.57), channel_id=1, source_target_pairs={{0,64},{8,72},{16,80},{24,88},{32,96},{40,104},{48,112},{56,120},{... | collective-permute-start | bytes 405512 | tf_op jit(solution)/shard_map/ppermute | solution.py:19
  242.4 4.9 %collective-permute-start.29 = (bf16[528,128]{1,0:T(8,128)(2,1)S(1)}, bf16[528,128]{1,0:T(8,128)(2,1)S(1)}, u32[]{:S(2)}, u32[]{:S(2)}) collective-permute-start(bf16[528,128]{1,0:T(8,128)(2,1)S(1)} %get-tuple-element.82), channel_id=1, source_target_pairs={{0,256},{8,264},{16,272},{24,280},{32,288},{40,296},{48,304},{56,3... | collective-permute-start | bytes 405512 | tf_op jit(solution)/shard_map/ppermute | solution.py:19
  248.6 2.4 collective-permute-start.28
  253.2 4.9 %collective-permute-start.27 = (bf16[528,128]{1,0:T(8,128)(2,1)S(1)}, bf16[528,128]{1,0:T(8,128)(2,1)S(1)}, u32[]{:S(2)}, u32[]{:S(2)}) collective-permute-start(bf16[528,128]{1,0:T(8,128)(2,1)S(1)} %get-tuple-element.76), channel_id=1, source_target_pairs={{0,256},{8,264},{16,272},{24,280},{32,288},{40,296},{48,304},{56,3... | collective-permute-start | bytes 405512 | tf_op jit(solution)/shard_map/ppermute | solution.py:19
  260.3 2.4 collective-permute-start.26
  264.0 4.9 %collective-permute-start.25 = (bf16[528,128]{1,0:T(8,128)(2,1)S(1)}, bf16[528,128]{1,0:T(8,128)(2,1)S(1)}, u32[]{:S(2)}, u32[]{:S(2)}) collective-permute-start(bf16[528,128]{1,0:T(8,128)(2,1)S(1)} %get-tuple-element.70), channel_id=1, source_target_pairs={{0,256},{8,264},{16,272},{24,280},{32,288},{40,296},{48,304},{56,3... | collective-permute-start | bytes 405512 | tf_op jit(solution)/shard_map/ppermute | solution.py:19
  270.1 2.6 collective-permute-start.16
  (135 shorter events, 80.4 us)
Async XLA Ops:
  6.5 78.5 %all-gather.5.cloned.1.call-start = ((), (), s32[]{:S(2)}) async-start(), calls=%async_computation | async-start | bytes 1966080 | tf_op jit(solution)/shard_map/all_gather | solution.py:147
  8.3 201.2 %all-gather.7.cloned.1.call-start = ((), (), s32[]{:S(2)}) async-start(), calls=%async_computation.1 | async-start | bytes 1310720 | tf_op jit(solution)/shard_map/all_gather | solution.py:148
  10.3 30.2 %collective-permute-start = (bf16[2,4,32,512]{3,2,1,0:T(8,128)(2,1)S(1)}, bf16[2,4,32,512]{3,2,1,0:T(8,128)(2,1)S(1)}, u32[]{:S(2)}, u32[]{:S(2)}) collective-permute-start(bf16[2,4,32,512]{3,2,1,0:T(8,128)(2,1)S(1)} %get-tuple-element.90), channel_id=1, source_target_pairs={{0,4},{4,0},{1,5},{5,1},{2,6},{6,2},{3,7},{7,3},{8,12},{12,8},{9,1... | collective-permute-start | bytes 786440 | tf_op jit(solution)/shard_map/ppermute | solution.py:19
  40.4 32.2 %collective-permute-start.1 = (bf16[2,4,32,512]{3,2,1,0:T(8,128)(2,1)S(1)}, bf16[2,4,32,512]{3,2,1,0:T(8,128)(2,1)S(1)}, u32[]{:S(2)}, u32[]{:S(2)}) collective-permute-start(bf16[2,4,32,512]{3,2,1,0:T(8,128)(2,1)S(1)} %get-tuple-element.47), channel_id=1, source_target_pairs={{0,4},{4,0},{1,5},{5,1},{2,6},{6,2},{3,7},{7,3},{8,12},{12,8},{9,1... | collective-permute-start | bytes 786440 | tf_op jit(solution)/shard_map/ppermute | solution.py:19
  42.7 38.3 %collective-permute-start.2 = (bf16[2,4,32,512]{3,2,1,0:T(8,128)(2,1)S(1)}, bf16[2,4,32,512]{3,2,1,0:T(8,128)(2,1)S(1)}, u32[]{:S(2)}, u32[]{:S(2)}) collective-permute-start(bf16[2,4,32,512]{3,2,1,0:T(8,128)(2,1)S(1)} %collective-permute-done.rest_0_), channel_id=1, source_target_pairs={{0,1},{1,2},{2,3},{3,0},{4,5},{5,6},{6,7},{7,4},{8,9},{9,10},{10,1... | collective-permute-start | bytes 786440 | tf_op jit(solution)/shard_map/ppermute | solution.py:144
  46.2 38.0 %collective-permute-start.3 = (bf16[2,4,32,512]{3,2,1,0:T(8,128)(2,1)S(1)}, bf16[2,4,32,512]{3,2,1,0:T(8,128)(2,1)S(1)}, u32[]{:S(2)}, u32[]{:S(2)}) collective-permute-start(bf16[2,4,32,512]{3,2,1,0:T(8,128)(2,1)S(1)} %collective-permute-done.rest_0_), channel_id=1, source_target_pairs={{0,2},{1,3},{2,0},{3,1},{4,6},{5,7},{6,4},{7,5},{8,10},{9,11},{10,... | collective-permute-start | bytes 786440 | tf_op jit(solution)/shard_map/ppermute | solution.py:144
  51.0 33.2 %collective-permute-start.4 = (bf16[2,4,32,512]{3,2,1,0:T(8,128)(2,1)S(1)}, bf16[2,4,32,512]{3,2,1,0:T(8,128)(2,1)S(1)}, u32[]{:S(2)}, u32[]{:S(2)}) collective-permute-start(bf16[2,4,32,512]{3,2,1,0:T(8,128)(2,1)S(1)} %collective-permute-done.rest_0_), channel_id=1, source_target_pairs={{0,3},{1,0},{2,1},{3,2},{4,7},{5,4},{6,5},{7,6},{8,11},{9,8},{10,9... | collective-permute-start | bytes 786440 | tf_op jit(solution)/shard_map/ppermute | solution.py:144
  72.7 19.3 %collective-permute-start.5 = (bf16[1,4,32,512]{3,2,1,0:T(8,128)(2,1)S(1)}, bf16[1,4,32,512]{3,2,1,0:T(8,128)(2,1)S(1)}, u32[]{:S(2)}, u32[]{:S(2)}) collective-permute-start(bf16[1,4,32,512]{3,2,1,0:T(8,128)(2,1)S(1)} %get-tuple-element.93.rest_0_), channel_id=1, source_target_pairs={{0,1},{1,2},{2,3},{3,0},{4,5},{5,6},{6,7},{7,4},{8,9},{9,10},{10,1... | collective-permute-start | bytes 393224 | tf_op jit(solution)/shard_map/ppermute | solution.py:144
  76.2 15.8 %collective-permute-start.6 = (bf16[1,4,32,512]{3,2,1,0:T(8,128)(2,1)S(1)}, bf16[1,4,32,512]{3,2,1,0:T(8,128)(2,1)S(1)}, u32[]{:S(2)}, u32[]{:S(2)}) collective-permute-start(bf16[1,4,32,512]{3,2,1,0:T(8,128)(2,1)S(1)} %get-tuple-element.93.rest_0_), channel_id=1, source_target_pairs={{0,2},{1,3},{2,0},{3,1},{4,6},{5,7},{6,4},{7,5},{8,10},{9,11},{10,... | collective-permute-start | bytes 393224 | tf_op jit(solution)/shard_map/ppermute | solution.py:144
  102.3 51.1 %collective-permute-start.21 = (bf16[528,128]{1,0:T(8,128)(2,1)S(1)}, bf16[528,128]{1,0:T(8,128)(2,1)S(1)}, u32[]{:S(2)}, u32[]{:S(2)}) collective-permute-start(bf16[528,128]{1,0:T(8,128)(2,1)S(1)} %get-tuple-element.65), channel_id=1, source_target_pairs={{0,64},{8,72},{16,80},{24,88},{32,96},{40,104},{48,112},{56,120},{... | collective-permute-start | bytes 405512 | tf_op jit(solution)/shard_map/ppermute | solution.py:19
  106.4 52.4 %collective-permute-start.9 = (bf16[528,128]{1,0:T(8,128)(2,1)S(1)}, bf16[528,128]{1,0:T(8,128)(2,1)S(1)}, u32[]{:S(2)}, u32[]{:S(2)}) collective-permute-start(bf16[528,128]{1,0:T(8,128)(2,1)S(1)} %get-tuple-element.54), channel_id=1, source_target_pairs={{0,64},{8,72},{16,80},{24,88},{32,96},{40,104},{48,112},{56,120},{... | collective-permute-start | bytes 405512 | tf_op jit(solution)/shard_map/ppermute | solution.py:19
  115.2 56.8 %collective-permute-start.17 = (bf16[1,4,32,512]{3,2,1,0:T(8,128)(2,1)S(1)}, bf16[1,4,32,512]{3,2,1,0:T(8,128)(2,1)}, u32[]{:S(2)}, u32[]{:S(2)}) collective-permute-start(bf16[1,4,32,512]{3,2,1,0:T(8,128)(2,1)S(1)} %slice.27), channel_id=1, source_target_pairs={{0,4},{4,0},{1,5},{5,1},{2,6},{6,2},{3,7},{7,3},{8,12},{12,8},{9,1... | collective-permute-start | bytes 393224 | tf_op jit(solution)/shard_map/ppermute | solution.py:19
  154.1 28.2 %collective-permute-start.22 = (bf16[528,128]{1,0:T(8,128)(2,1)S(1)}, bf16[528,128]{1,0:T(8,128)(2,1)S(1)}, u32[]{:S(2)}, u32[]{:S(2)}) collective-permute-start(bf16[528,128]{1,0:T(8,128)(2,1)S(1)} %get-tuple-element.66), channel_id=1, source_target_pairs={{0,64},{8,72},{16,80},{24,88},{32,96},{40,104},{48,112},{56,120},{... | collective-permute-start | bytes 405512 | tf_op jit(solution)/shard_map/ppermute | solution.py:19
  158.9 29.3 %collective-permute-start.10 = (bf16[528,128]{1,0:T(8,128)(2,1)S(1)}, bf16[528,128]{1,0:T(8,128)(2,1)S(1)}, u32[]{:S(2)}, u32[]{:S(2)}) collective-permute-start(bf16[528,128]{1,0:T(8,128)(2,1)S(1)} %get-tuple-element.55), channel_id=1, source_target_pairs={{0,64},{8,72},{16,80},{24,88},{32,96},{40,104},{48,112},{56,120},{... | collective-permute-start | bytes 405512 | tf_op jit(solution)/shard_map/ppermute | solution.py:19
  166.7 26.9 %collective-permute-start.13 = (bf16[1,4,32,512]{3,2,1,0:T(8,128)(2,1)S(1)}, bf16[1,4,32,512]{3,2,1,0:T(8,128)(2,1)S(1)}, u32[]{:S(2)}, u32[]{:S(2)}) collective-permute-start(bf16[1,4,32,512]{3,2,1,0:T(8,128)(2,1)S(1)} %get-tuple-element.92.rest_0_), channel_id=1, source_target_pairs={{0,1},{1,2},{2,3},{3,0},{4,5},{5,6},{6,7},{7,4},{8,9},{9,10},{10,1... | collective-permute-start | bytes 393224 | tf_op jit(solution)/shard_map/ppermute | solution.py:144
  169.3 32.1 %collective-permute-start.14 = (bf16[1,4,32,512]{3,2,1,0:T(8,128)(2,1)S(1)}, bf16[1,4,32,512]{3,2,1,0:T(8,128)(2,1)S(1)}, u32[]{:S(2)}, u32[]{:S(2)}) collective-permute-start(bf16[1,4,32,512]{3,2,1,0:T(8,128)(2,1)S(1)} %get-tuple-element.92.rest_0_), channel_id=1, source_target_pairs={{0,2},{1,3},{2,0},{3,1},{4,6},{5,7},{6,4},{7,5},{8,10},{9,11},{10,... | collective-permute-start | bytes 393224 | tf_op jit(solution)/shard_map/ppermute | solution.py:144
  172.0 34.1 %collective-permute-start.15 = (bf16[1,4,32,512]{3,2,1,0:T(8,128)(2,1)S(1)}, bf16[1,4,32,512]{3,2,1,0:T(8,128)(2,1)S(1)}, u32[]{:S(2)}, u32[]{:S(2)}) collective-permute-start(bf16[1,4,32,512]{3,2,1,0:T(8,128)(2,1)S(1)} %get-tuple-element.92.rest_0_), channel_id=1, source_target_pairs={{0,3},{1,0},{2,1},{3,2},{4,7},{5,4},{6,5},{7,6},{8,11},{9,8},{10,9... | collective-permute-start | bytes 393224 | tf_op jit(solution)/shard_map/ppermute | solution.py:144
  182.2 34.0 %collective-permute-start.18 = (bf16[1,4,32,512]{3,2,1,0:T(8,128)(2,1)}, bf16[1,4,32,512]{3,2,1,0:T(8,128)(2,1)}, u32[]{:S(2)}, u32[]{:S(2)}) collective-permute-start(bf16[1,4,32,512]{3,2,1,0:T(8,128)(2,1)} %collective-permute-done.17.rest_0_), channel_id=1, source_target_pairs={{0,1},{1,2},{2,3},{3,0},{4,5},{5,6},{6,7},{7,4},{8,9},{9,10},{10,1... | collective-permute-start | bytes 393224 | tf_op jit(solution)/shard_map/ppermute | solution.py:144
  188.1 36.2 %collective-permute-start.23 = (bf16[528,128]{1,0:T(8,128)(2,1)}, bf16[528,128]{1,0:T(8,128)(2,1)}, u32[]{:S(2)}, u32[]{:S(2)}) collective-permute-start(bf16[528,128]{1,0:T(8,128)(2,1)} %get-tuple-element.67), channel_id=1, source_target_pairs={{0,64},{8,72},{16,80},{24,88},{32,96},{40,104},{48,112},{56,120},{... | collective-permute-start | bytes 405512 | tf_op jit(solution)/shard_map/ppermute | solution.py:19
  193.6 35.3 %collective-permute-start.11 = (bf16[528,128]{1,0:T(8,128)(2,1)}, bf16[528,128]{1,0:T(8,128)(2,1)}, u32[]{:S(2)}, u32[]{:S(2)}) collective-permute-start(bf16[528,128]{1,0:T(8,128)(2,1)} %get-tuple-element.56), channel_id=1, source_target_pairs={{0,64},{8,72},{16,80},{24,88},{32,96},{40,104},{48,112},{56,120},{... | collective-permute-start | bytes 405512 | tf_op jit(solution)/shard_map/ppermute | solution.py:19
  202.1 31.1 %collective-permute-start.19 = (bf16[1,4,32,512]{3,2,1,0:T(8,128)(2,1)}, bf16[1,4,32,512]{3,2,1,0:T(8,128)(2,1)}, u32[]{:S(2)}, u32[]{:S(2)}) collective-permute-start(bf16[1,4,32,512]{3,2,1,0:T(8,128)(2,1)} %collective-permute-done.17.rest_0_), channel_id=1, source_target_pairs={{0,2},{1,3},{2,0},{3,1},{4,6},{5,7},{6,4},{7,5},{8,10},{9,11},{10,... | collective-permute-start | bytes 393224 | tf_op jit(solution)/shard_map/ppermute | solution.py:144
  206.7 35.7 %collective-permute-start.20 = (bf16[1,4,32,512]{3,2,1,0:T(8,128)(2,1)}, bf16[1,4,32,512]{3,2,1,0:T(8,128)(2,1)}, u32[]{:S(2)}, u32[]{:S(2)}) collective-permute-start(bf16[1,4,32,512]{3,2,1,0:T(8,128)(2,1)} %collective-permute-done.17.rest_0_), channel_id=1, source_target_pairs={{0,3},{1,0},{2,1},{3,2},{4,7},{5,4},{6,5},{7,6},{8,11},{9,8},{10,9... | collective-permute-start | bytes 393224 | tf_op jit(solution)/shard_map/ppermute | solution.py:144
  216.3 32.3 %collective-permute-start.30 = (bf16[528,128]{1,0:T(8,128)(2,1)S(1)}, bf16[528,128]{1,0:T(8,128)(2,1)S(1)}, u32[]{:S(2)}, u32[]{:S(2)}) collective-permute-start(bf16[528,128]{1,0:T(8,128)(2,1)S(1)} %get-tuple-element.85), channel_id=1, source_target_pairs={{0,256},{8,264},{16,272},{24,280},{32,288},{40,296},{48,304},{56,3... | collective-permute-start | bytes 405512 | tf_op jit(solution)/shard_map/ppermute | solution.py:19
  224.3 28.9 %collective-permute-start.31 = (bf16[528,128]{1,0:T(8,128)(2,1)S(1)}, bf16[528,128]{1,0:T(8,128)(2,1)S(1)}, u32[]{:S(2)}, u32[]{:S(2)}) collective-permute-start(bf16[528,128]{1,0:T(8,128)(2,1)S(1)} %get-tuple-element.88), channel_id=1, source_target_pairs={{0,256},{8,264},{16,272},{24,280},{32,288},{40,296},{48,304},{56,3... | collective-permute-start | bytes 405512 | tf_op jit(solution)/shard_map/ppermute | solution.py:19
  228.9 31.3 %collective-permute-start.24 = (bf16[528,128]{1,0:T(8,128)(2,1)S(1)}, bf16[528,128]{1,0:T(8,128)(2,1)S(1)}, u32[]{:S(2)}, u32[]{:S(2)}) collective-permute-start(bf16[528,128]{1,0:T(8,128)(2,1)S(1)} %get-tuple-element.68), channel_id=1, source_target_pairs={{0,64},{8,72},{16,80},{24,88},{32,96},{40,104},{48,112},{56,120},{... | collective-permute-start | bytes 405512 | tf_op jit(solution)/shard_map/ppermute | solution.py:19
  233.2 30.8 %collective-permute-start.12 = (bf16[528,128]{1,0:T(8,128)(2,1)S(1)}, bf16[528,128]{1,0:T(8,128)(2,1)S(1)}, u32[]{:S(2)}, u32[]{:S(2)}) collective-permute-start(bf16[528,128]{1,0:T(8,128)(2,1)S(1)} %get-tuple-element.57), channel_id=1, source_target_pairs={{0,64},{8,72},{16,80},{24,88},{32,96},{40,104},{48,112},{56,120},{... | collective-permute-start | bytes 405512 | tf_op jit(solution)/shard_map/ppermute | solution.py:19
  242.4 27.7 %collective-permute-start.29 = (bf16[528,128]{1,0:T(8,128)(2,1)S(1)}, bf16[528,128]{1,0:T(8,128)(2,1)S(1)}, u32[]{:S(2)}, u32[]{:S(2)}) collective-permute-start(bf16[528,128]{1,0:T(8,128)(2,1)S(1)} %get-tuple-element.82), channel_id=1, source_target_pairs={{0,256},{8,264},{16,272},{24,280},{32,288},{40,296},{48,304},{56,3... | collective-permute-start | bytes 405512 | tf_op jit(solution)/shard_map/ppermute | solution.py:19
  248.6 31.1 %collective-permute-start.28 = (bf16[528,128]{1,0:T(8,128)(2,1)S(1)}, bf16[528,128]{1,0:T(8,128)(2,1)S(1)}, u32[]{:S(2)}, u32[]{:S(2)}) collective-permute-start(bf16[528,128]{1,0:T(8,128)(2,1)S(1)} %get-tuple-element.79), channel_id=1, source_target_pairs={{0,256},{8,264},{16,272},{24,280},{32,288},{40,296},{48,304},{56,3... | collective-permute-start | bytes 405512 | tf_op jit(solution)/shard_map/ppermute | solution.py:19
  253.2 28.2 %collective-permute-start.27 = (bf16[528,128]{1,0:T(8,128)(2,1)S(1)}, bf16[528,128]{1,0:T(8,128)(2,1)S(1)}, u32[]{:S(2)}, u32[]{:S(2)}) collective-permute-start(bf16[528,128]{1,0:T(8,128)(2,1)S(1)} %get-tuple-element.76), channel_id=1, source_target_pairs={{0,256},{8,264},{16,272},{24,280},{32,288},{40,296},{48,304},{56,3... | collective-permute-start | bytes 405512 | tf_op jit(solution)/shard_map/ppermute | solution.py:19
  260.3 22.9 %collective-permute-start.26 = (bf16[528,128]{1,0:T(8,128)(2,1)S(1)}, bf16[528,128]{1,0:T(8,128)(2,1)S(1)}, u32[]{:S(2)}, u32[]{:S(2)}) collective-permute-start(bf16[528,128]{1,0:T(8,128)(2,1)S(1)} %get-tuple-element.73), channel_id=1, source_target_pairs={{0,256},{8,264},{16,272},{24,280},{32,288},{40,296},{48,304},{56,3... | collective-permute-start | bytes 405512 | tf_op jit(solution)/shard_map/ppermute | solution.py:19
  264.0 21.0 %collective-permute-start.25 = (bf16[528,128]{1,0:T(8,128)(2,1)S(1)}, bf16[528,128]{1,0:T(8,128)(2,1)S(1)}, u32[]{:S(2)}, u32[]{:S(2)}) collective-permute-start(bf16[528,128]{1,0:T(8,128)(2,1)S(1)} %get-tuple-element.70), channel_id=1, source_target_pairs={{0,256},{8,264},{16,272},{24,280},{32,288},{40,296},{48,304},{56,3... | collective-permute-start | bytes 405512 | tf_op jit(solution)/shard_map/ppermute | solution.py:19
  270.1 16.5 %collective-permute-start.16 = (bf16[528,128]{1,0:T(8,128)(2,1)S(1)}, bf16[528,128]{1,0:T(8,128)(2,1)S(1)}, u32[]{:S(2)}, u32[]{:S(2)}) collective-permute-start(bf16[528,128]{1,0:T(8,128)(2,1)S(1)} %get-tuple-element.59), channel_id=1, source_target_pairs={{0,256},{8,264},{16,272},{24,280},{32,288},{40,296},{48,304},{56,3... | collective-permute-start | bytes 405512 | tf_op jit(solution)/shard_map/ppermute | solution.py:19
  (34 other events, 172.5 us)
Sparse Core Ops, SparseCore 0:
  9.5 33.2 all-gather.4
  95.4 29.6 all-gather.6

commit v3 on v2

--- a/solution.py
+++ b/solution.py
@@ -19,15 +19,19 @@
     return lax.ppermute(shard, axis, [(i, i ^ 1 << apart) for i in range(lax.axis_size(axis))])
 
 
-def assemble(matrix, level, own_ref, other_refs, half, part):
-    parts, _, blocks, rows, _ = own_ref.shape
-    for block in range(blocks):
-        for k in range(parts):
-            start = pl.multiple_of((half * parts + k) * rows, rows)
-            matrix[level, block, pl.ds(start, rows), :] = own_ref[k, level, block]
-            place = (1 - half) * parts + ((part + (parts - k)) & (parts - 1))
-            start = pl.multiple_of(place * rows, rows)
-            matrix[level, block, pl.ds(start, rows), :] = other_refs[k][level, block]
+def assembling(pairs, sems, half):
+    copies = []
+    for own_ref, other_ref, at, matrix_ref in pairs:
+        parts, _, _, rows, _ = own_ref.shape
+        for part in range(parts):
+            for ref, side in ((own_ref, half), (other_ref, 1 - half)):
+                start = pl.multiple_of((side * parts + part) * rows, rows)
+                copies.append(
+                    pltpu.make_async_copy(
+                        ref.at[part, at], matrix_ref.at[:, pl.ds(start, rows), :], sems.at[len(copies)]
+                    )
+                )
+    return copies
 
 
 def split(x):
@@ -75,12 +79,17 @@
     return [split(value[:, k * size:(k + 1) * size]) for k in range(count)]
 
 
-def local_body(bits_ref, x_ref, own, *rest):
-    others, out_ref, matrix = rest[:-2], rest[-2], rest[-1]
+def local_body(bits_ref, x_ref, own, other, out_ref, next_ref, matrix, sems):
     levels, count, size = matrix.shape[:3]
+    pairs = [(own, other, level, matrix.at[level]) for level in range(levels)] + [(own, other, levels, next_ref)]
+    copies = assembling(pairs, sems, bits_ref[0])
+    each = len(copies) // len(pairs)
+    for copy in copies:
+        copy.start()
     value = x_ref[...]
     for level in range(levels):
-        assemble(matrix, level, own, others, bits_ref[0], bits_ref[1])
+        for copy in copies[level * each:(level + 1) * each]:
+            copy.wait()
         parts = blocks_of(value, count, size)
         outs = []
         for k in range(count):
@@ -90,22 +99,29 @@
             )
         value = jnp.concatenate(outs, axis=1)
     out_ref[...] = value
-
-
-def prepare_body(bits_ref, own, *rest):
-    assemble(rest[-1], 0, own, rest[:-1], bits_ref[0], bits_ref[1])
+    for copy in copies[levels * each:]:
+        copy.wait()
+
+
+def prepare_body(bits_ref, own, other, *rest):
+    outs, sems = rest[:-1], rest[-1]
+    copies = assembling([(own, other, at, ref) for at, ref in enumerate(outs)], sems, bits_ref[0])
+    for copy in copies:
+        copy.start()
+    for copy in copies:
+        copy.wait()
 
 
 def cross_level(mine, partner, matrix, upper):
-    _, count, size, _ = matrix.shape
+    count, size, _ = matrix.shape
     own_parts, partner_parts = blocks_of(mine, count, size), blocks_of(partner, count, size)
     own_at = pl.multiple_of(upper * size, size)
     partner_at = pl.multiple_of((1 - upper) * size, size)
     outs = []
     for k in range(count):
         outs.append(
-            product(own_parts[k], matrix[0, k, :, pl.ds(own_at, size)])
-            + product(partner_parts[k], matrix[0, k, :, pl.ds(partner_at, size)])
+            product(own_parts[k], matrix[k, :, pl.ds(own_at, size)])
+            + product(partner_parts[k], matrix[k, :, pl.ds(partner_at, size)])
         )
     return jnp.concatenate(outs, axis=1)
 
@@ -126,7 +142,7 @@
     rest[-1][...] = cross_level(mine_ref[...], decode(partner_ref, *mine_ref.shape), matrix, bits_ref[4])
 
 
-def on_device(vectors, weights, chunks=8, window=2):
+def on_device(vectors, weights, chunks=4, window=2):
     columns, coeffs = vectors.shape
     _, count, share, width = weights.shape
     parts = lax.axis_size("narrow_1")
@@ -140,19 +156,15 @@
     )
 
     def around(shard):
-        return [shard] + [
-            lax.ppermute(shard, "narrow_1", [(i, (i + k) % parts) for i in range(parts)]) for k in range(1, parts)
-        ]
-
-    own_early = lax.all_gather(weights[:3], "narrow_1")
-    own_late = lax.all_gather(weights[3:], "narrow_1")
-    first = swapped(weights[:2], "narrow_0", 0)
-    turn, _ = lax.optimization_barrier((weights[2:4], first))
-    second = swapped(turn, "narrow_0", 0)
-    turn, _ = lax.optimization_barrier((weights[4:], second))
-    third = swapped(turn, "narrow_0", 0)
-    vectors, _ = lax.optimization_barrier((vectors, second))
-    others = [around(first), around(second[:1]), around(second[1:]), around(third)]
+        return lax.all_to_all(jnp.broadcast_to(shard[None], (parts,) + shard.shape), "narrow_1", 0, 0)
+
+    early, late = lax.optimization_barrier((weights[:3], weights[3:]))
+    own_early = lax.all_gather(early, "narrow_1")
+    own_late = lax.all_gather(late, "narrow_1")
+    early_other = swapped(early, "narrow_0", 0)
+    late_turn, _ = lax.optimization_barrier((late, early_other))
+    late_other = swapped(late_turn, "narrow_0", 0)
+    other_early = around(early_other)
 
     def call(body, in_specs, out_specs, out_shape, scratch, estimate, aliases={}):
         return pl.pallas_call(
@@ -173,60 +185,62 @@
 
     size = width // 2
     matrix_bytes = 2 * count * size * width
-    matrix_shape = (1, count, size, width)
-
-    def gathered_spec(levels, at):
-        return pl.BlockSpec((parts, levels, count, share, width), lambda i, bits: (0, at, 0, 0, 0))
-
-    def shard_spec(levels, at):
-        return pl.BlockSpec((levels, count, share, width), lambda i, bits: (at, 0, 0, 0))
-
-    def prepared(own, own_at, other, other_at):
-        return call(
-            prepare_body, [gathered_spec(1, own_at)] + [shard_spec(1, other_at)] * parts,
-            pl.BlockSpec(matrix_shape, lambda i, bits: (0, 0, 0, 0)),
-            jax.ShapeDtypeStruct(matrix_shape, weights.dtype), [], cost(0, 0, 2 * matrix_bytes),
-        )(bits, own, *other)
+    matrix_shape = (count, size, width)
 
     def row_spec(index):
         return pl.BlockSpec((rows, coeffs), lambda i, bits: (index, 0))
 
-    matrix_spec = pl.BlockSpec(matrix_shape, lambda i, bits: (0, 0, 0, 0))
+    matrix_spec = pl.BlockSpec(matrix_shape, lambda i, bits: (0, 0, 0))
+    anywhere = pl.BlockSpec(memory_space=pl.ANY)
+    matrix_type = jax.ShapeDtypeStruct(matrix_shape, weights.dtype)
     full = pl.BlockSpec((columns, coeffs), lambda i, bits: (0, 0))
     code_spec = pl.BlockSpec((code_rows, LANES), lambda i, bits: (0, 0))
     code_shape = jax.ShapeDtypeStruct((code_rows, LANES), jnp.bfloat16)
     chunk_shape = jax.ShapeDtypeStruct((rows, coeffs), jnp.float32)
     full_shape = jax.ShapeDtypeStruct((columns, coeffs), jnp.float32)
 
-    current = call(
-        local_body, [full, gathered_spec(2, 0)] + [shard_spec(2, 0)] * parts, full, full_shape,
-        [pltpu.VMEM((2,) + matrix_shape[1:], weights.dtype)], cost(columns, 2, 8 * columns * coeffs + 2 * matrix_bytes),
-    )(bits, vectors, own_early, *others[0])
-    sent, _ = lax.optimization_barrier((current, others[1]))
+    current, matrix = call(
+        local_body, [full, anywhere, anywhere], [full, anywhere], [full_shape, matrix_type],
+        [pltpu.VMEM((2,) + matrix_shape, weights.dtype), pltpu.SemaphoreType.DMA((6 * parts,))],
+        cost(columns, 2, 8 * columns * coeffs + 4 * matrix_bytes),
+    )(bits, vectors, own_early, other_early)
+    sent, late_other = lax.optimization_barrier((current, late_other))
     partner = swapped(sent, "wide", wide_bits[0])
-    matrix = prepared(own_early, 2, others[1], 0)
-
-    pieces = []
+    other_late = around(late_other)
+
+    owns, codes = [], []
     for c in range(chunks):
         mine, code = call(
             core_body, [row_spec(c), row_spec(c), matrix_spec], [row_spec(0), code_spec],
             [chunk_shape, code_shape], [], cost(rows, 1, 14 * rows * coeffs + matrix_bytes),
         )(bits, current, partner, matrix)
-        if c >= window:
-            code, _ = lax.optimization_barrier((code, pieces[c - window][1]))
-        pieces.append((mine, swapped(code, "wide", wide_bits[1])))
-    matrix = prepared(own_late, 0, others[2], 0)
-    later = []
-    for mine, code in pieces:
+        owns.append(mine)
+        codes.append(code)
+    arrived, later = [], []
+
+    def middle(c):
         mine, code = call(
             middle_body, [row_spec(0), code_spec, matrix_spec], [row_spec(0), code_spec],
             [chunk_shape, code_shape], [], cost(rows, 1, 12 * rows * coeffs + matrix_bytes),
-        )(bits, mine, code, matrix)
-        later.append((mine, swapped(code, "wide", wide_bits[2])))
-    matrix = prepared(own_late, 1, others[3], 0)
+        )(bits, owns[c], arrived[c], middle_matrix)
+        later.append((mine, code, swapped(code, "wide", wide_bits[2])))
+
+    for c in range(chunks):
+        code = codes[c]
+        if c >= window:
+            code, _ = lax.optimization_barrier((code, [arrived[c - window], codes[-1]]))
+        arrived.append(swapped(code, "wide", wide_bits[1]))
+    own_late, other_late, _ = lax.optimization_barrier((own_late, other_late, arrived[window - 1]))
+    middle_matrix, last_matrix = call(
+        prepare_body, [anywhere] * 2, [anywhere] * 2, [matrix_type] * 2, [pltpu.SemaphoreType.DMA((4 * parts,))],
+        cost(0, 0, 4 * matrix_bytes),
+    )(bits, own_late, other_late)
+    for c in range(chunks):
+        middle(c)
+    later = [(mine, code) for mine, _, code in later]
     out = None
     for c, (mine, code) in enumerate(later):
-        operands = [bits, mine, code, matrix]
+        operands = [bits, mine, code, last_matrix]
         specs = [row_spec(0), code_spec, matrix_spec]
         if out is not None:
             operands.append(out)

time: 297 us -> 237 us (0.80)
  starting transfers between devices: 123 us -> 48 us
  waiting for transfers between devices: 82.5 us -> 123 us
  Pallas kernels: 51.8 us -> 33.7 us
  local copies, waits for them, and re-layouts: 24.4 us -> 14.9 us
    ppermute x20 -> x11, starting transfers between devices: 81.2 us -> 38.9 us  [swapped(): lax.ppermute(shard, axis, [(i, i ^ 1 << apart) for i in range(lax.axis_si...]
    ppermute x12 -> x0, starting transfers between devices: 41.3 us -> none  [around(): lax.ppermute(shard, 'narrow_1', [(i, (i + k) % parts) for i in range(part...]
    ppermute x20 -> x11, waiting for transfers between devices: 82.4 us -> 105 us  [swapped(): lax.ppermute(shard, axis, [(i, i ^ 1 << apart) for i in range(lax.axis_si...]
    all_to_all x0 -> x2, waiting for transfers between devices: none -> 18.2 us  [around(): lax.all_to_all(jnp.broadcast_to(shard[None], (parts,) + shard.shape), 'na...]
    unnamed x64 -> x28, local copies, waits for them, and re-layouts: 19.7 us -> 8.63 us
    all_to_all x0 -> x2, starting transfers between devices: none -> 9.12 us  [around(): lax.all_to_all(jnp.broadcast_to(shard[None], (parts,) + shard.shape), 'na...]
    pallas_call x8 -> x4, Pallas kernels: 18.7 us -> 10.8 us  [on_device(): call(core_body, [row_spec(c), row_spec(c), matrix_spec], [row_spec(0), co...]
    pallas_call x8 -> x4, Pallas kernels: 13.9 us -> 7.72 us  [on_device(): call(last_body, specs, row_spec(c), full_shape, [], cost(rows, 1, 10 * ro...]
  transfers between devices with their start and end apart: 34 -> 15, of which waited for: 5 -> 7; matrix products, arithmetic and copies ran while one was open for 1% -> 1% of each run, Pallas kernels for 17% -> 14%
where the time goes in v3:
time: 237 us; the launch traced here: 233 us
  waiting for transfers between devices  123 us (52%)
  starting transfers between devices  48 us (20%)
  Pallas kernels  33.7 us (14%)
  local copies, waits for them, and re-layouts  14.9 us (6%)
  between operations  13.7 us (6%)
    ppermute x11, waiting for transfers between devices, swapped(): lax.ppermute(shard, axis, [(i, i ^ 1 << apart) for i in range(lax.axis_si...  105 us
    ppermute x11, starting transfers between devices, swapped(): lax.ppermute(shard, axis, [(i, i ^ 1 << apart) for i in range(lax.axis_si...  38.9 us
    all_to_all x2, waiting for transfers between devices, around(): lax.all_to_all(jnp.broadcast_to(shard[None], (parts,) + shard.shape), 'na...  18.2 us
    pallas_call x4, Pallas kernels, on_device(): call(core_body, [row_spec(c), row_spec(c), matrix_spec], [row_spec(0), co...  10.8 us
    all_to_all x2, starting transfers between devices, around(): lax.all_to_all(jnp.broadcast_to(shard[None], (parts,) + shard.shape), 'na...  9.12 us
    unnamed x28, local copies, waits for them, and re-layouts  8.63 us
    pallas_call x4, Pallas kernels, on_device(): call(last_body, specs, row_spec(c), full_shape, [], cost(rows, 1, 10 * ro...  7.72 us
    pallas_call x1, Pallas kernels, on_device(): call(local_body, [full, anywhere, anywhere], [full, anywhere], [full_shap...  7.41 us
  transfers between devices with their start and end apart: 15, of which 7 were waited for; matrix products, arithmetic and copies ran while one was open for 1% of the time, Pallas kernels for 14%

profile of v3, /device:TPU:480, one launch (start us, length us, event | category | flops | bytes accessed | tf_op | source)
XLA Modules:
  0.0 233.4 jit_solution(1460159258070911875)
XLA Ops:
  7.5 1.9 slice.6
  9.4 6.3 %collective-permute-start = (bf16[3,4,32,512]{3,2,1,0:T(8,128)(2,1)}, bf16[3,4,32,512]{3,2,1,0:T(8,128)(2,1)S(1)}, u32[]{:S(2)}, u32[]{:S(2)}) collective-permute-start(bf16[3,4,32,512]{3,2,1,0:T(8,128)(2,1)} %slice.6), channel_id=1, source_target_pairs={{0,4},{4,0},{1,5},{5,1},{2,6},{6,2},{3,7},{7,3},{8,12},{12,8},{9,1... | collective-permute-start | bytes 1179656 | tf_op jit(solution)/shard_map/ppermute | solution.py:19
  15.7 34.1 %collective-permute-done = bf16[3,4,32,512]{3,2,1,0:T(8,128)(2,1)S(1)} collective-permute-done((bf16[3,4,32,512]{3,2,1,0:T(8,128)(2,1)}, bf16[3,4,32,512]{3,2,1,0:T(8,128)(2,1)S(1)}, u32[]{:S(2)}, u32[]{:S(2)}) %collective-permute-start) | collective-permute-done | bytes 393248 | tf_op jit(solution)/shard_map/ppermute | solution.py:19
  51.1 4.5 %all-to-all-start = ((bf16[4,3,4,32,512]{4,3,2,1,0:T(8,128)(2,1)}), bf16[4,3,4,32,512]{4,3,2,1,0:T(8,128)(2,1)S(1)}, u32[]{:S(2)}, u32[]{:S(2)}) async-start(bf16[4,3,4,32,512]{4,3,2,1,0:T(8,128)(2,1)} %broadcast_in_dim.4), calls=%async_computation | async-start | bytes 3145728 | tf_op jit(solution)/shard_map/all_to_all | solution.py:159
  55.6 2.3 collective-permute-start.1
  58.0 18.2 %all-to-all-done.other = bf16[4,3,4,32,512]{4,3,2,1,0:T(8,128)(2,1)S(1)} async-done(((bf16[4,3,4,32,512]{4,3,2,1,0:T(8,128)(2,1)}), bf16[4,3,4,32,512]{4,3,2,1,0:T(8,128)(2,1)S(1)}, u32[]{:S(2)}, u32[]{:S(2)}) %all-to-all-start) | async-done | bytes 1572896 | tf_op jit(solution)/shard_map/all_to_all | solution.py:159
  77.6 7.4 %shard_map.28 = (f32[512,1024]{1,0:T(8,128)}, bf16[4,256,512]{2,1,0:T(8,128)(2,1)S(1)}) custom-call(s32[5]{0:T(128)S(1)} %stack.23.bits_ref, f32[512,1024]{1,0:T(8,128)} %x_ref.1, bf16[4,3,4,32,512]{4,3,2,1,0:T(8,128)(2,1)S(1)} %bitcast.8, bf16[4,3,4,32,512]{4,3,2,1,0:T(8,128)(2,1)S(1)} %all-to-all-done.other), custom_call_target="tpu_custom_call" | custom-call | flops 2147483648 | bytes 8388608 | tf_op jit(solution)/shard_map/pallas_call | solution.py:202
  86.2 1.9 collective-permute-start.2
  88.1 2.1 broadcast_in_dim.5
  90.2 4.7 %all-to-all-start.1 = ((bf16[4,2,4,32,512]{4,3,2,1,0:T(8,128)(2,1)}), bf16[4,2,4,32,512]{4,3,2,1,0:T(8,128)(2,1)}, u32[]{:S(2)}, u32[]{:S(2)}) async-start(bf16[4,2,4,32,512]{4,3,2,1,0:T(8,128)(2,1)} %broadcast_in_dim.5), calls=%async_computation.1 | async-start | bytes 2097152 | tf_op jit(solution)/shard_map/all_to_all | solution.py:159
  94.9 2.3 %shard_map.34 = (f32[128,1024]{1,0:T(8,128)S(1)}, bf16[1040,128]{1,0:T(8,128)(2,1)S(1)}) custom-call(s32[5]{0:T(128)S(1)} %stack.23.bits_ref, f32[512,1024]{1,0:T(8,128)S(1)} %copy-done, f32[512,1024]{1,0:T(8,128)} %collective-permute-done.2.partner_ref, bf16[4,256,512]{2,1,0:T(8,128)(2,1)S(1)} %get-tuple-element.39.matrix), custom_call_target="tpu_custom_call" | custom-call | flops 268435456 | bytes 2883584 | tf_op jit(solution)/shard_map/pallas_call | solution.py:213
  98.0 7.4 %collective-permute-start.6 = (bf16[1040,128]{1,0:T(8,128)(2,1)S(1)}, bf16[1040,128]{1,0:T(8,128)(2,1)S(1)}, u32[]{:S(2)}, u32[]{:S(2)}) collective-permute-start(bf16[1040,128]{1,0:T(8,128)(2,1)S(1)} %get-tuple-element.53), channel_id=1, source_target_pairs={{0,64},{8,72},{16,80},{24,88},{32,96},{40,104},{48,112},{56,120},{... | collective-permute-start | bytes 798728 | tf_op jit(solution)/shard_map/ppermute | solution.py:19
  105.4 2.4 %shard_map.30 = (f32[128,1024]{1,0:T(8,128)S(1)}, bf16[1040,128]{1,0:T(8,128)(2,1)S(1)}) custom-call(s32[5]{0:T(128)S(1)} %stack.23.bits_ref, f32[512,1024]{1,0:T(8,128)S(1)} %copy-done, f32[512,1024]{1,0:T(8,128)} %collective-permute-done.2.partner_ref, bf16[4,256,512]{2,1,0:T(8,128)(2,1)S(1)} %get-tuple-element.39.matrix), custom_call_target="tpu_custom_call" | custom-call | flops 268435456 | bytes 2883584 | tf_op jit(solution)/shard_map/pallas_call | solution.py:213
  108.6 2.3 collective-permute-start.3
  110.9 3.1 %shard_map.33 = (f32[128,1024]{1,0:T(8,128)S(1)}, bf16[1040,128]{1,0:T(8,128)(2,1)}) custom-call(s32[5]{0:T(128)S(1)} %stack.23.bits_ref, f32[512,1024]{1,0:T(8,128)S(1)} %copy-done, f32[512,1024]{1,0:T(8,128)} %collective-permute-done.2.partner_ref, bf16[4,256,512]{2,1,0:T(8,128)(2,1)S(1)} %get-tuple-element.39.matrix), custom_call_target="tpu_custom_call" | custom-call | flops 268435456 | bytes 2883584 | tf_op jit(solution)/shard_map/pallas_call | solution.py:213
  114.8 3.0 %shard_map.29 = (f32[128,1024]{1,0:T(8,128)S(1)}, bf16[1040,128]{1,0:T(8,128)(2,1)}) custom-call(s32[5]{0:T(128)S(1)} %stack.23.bits_ref, f32[512,1024]{1,0:T(8,128)S(1)} %copy-done, f32[512,1024]{1,0:T(8,128)} %collective-permute-done.2.partner_ref, bf16[4,256,512]{2,1,0:T(8,128)(2,1)S(1)} %get-tuple-element.39.matrix), custom_call_target="tpu_custom_call" | custom-call | flops 268435456 | bytes 2883584 | tf_op jit(solution)/shard_map/pallas_call | solution.py:213
  118.6 56.6 %collective-permute-done.6.partner_ref = bf16[1040,128]{1,0:T(8,128)(2,1)S(1)} collective-permute-done((bf16[1040,128]{1,0:T(8,128)(2,1)S(1)}, bf16[1040,128]{1,0:T(8,128)(2,1)S(1)}, u32[]{:S(2)}, u32[]{:S(2)}) %collective-permute-start.6) | collective-permute-done | bytes 266272 | tf_op jit(solution)/shard_map/ppermute | solution.py:19
  175.9 1.9 collective-permute-start.7
  177.8 8.8 %collective-permute-done.3.partner_ref = bf16[1040,128]{1,0:T(8,128)(2,1)S(1)} collective-permute-done((bf16[1040,128]{1,0:T(8,128)(2,1)S(1)}, bf16[1040,128]{1,0:T(8,128)(2,1)S(1)}, u32[]{:S(2)}, u32[]{:S(2)}) %collective-permute-start.3) | collective-permute-done | bytes 266272 | tf_op jit(solution)/shard_map/ppermute | solution.py:19
  186.6 1.9 collective-permute-start.4
  189.8 2.1 shard_map.31
  194.4 5.1 %collective-permute-start.10 = (bf16[1040,128]{1,0:T(8,128)(2,1)S(1)}, bf16[1040,128]{1,0:T(8,128)(2,1)S(1)}, u32[]{:S(2)}, u32[]{:S(2)}) collective-permute-start(bf16[1040,128]{1,0:T(8,128)(2,1)S(1)} %get-tuple-element.62), channel_id=1, source_target_pairs={{0,256},{8,264},{16,272},{24,280},{32,288},{40,296},{48,304},{56,3... | collective-permute-start | bytes 798728 | tf_op jit(solution)/shard_map/ppermute | solution.py:19
  202.0 2.4 %collective-permute-start.9 = (bf16[1040,128]{1,0:T(8,128)(2,1)S(1)}, bf16[1040,128]{1,0:T(8,128)(2,1)S(1)}, u32[]{:S(2)}, u32[]{:S(2)}) collective-permute-start(bf16[1040,128]{1,0:T(8,128)(2,1)S(1)} %get-tuple-element.59), channel_id=1, source_target_pairs={{0,256},{8,264},{16,272},{24,280},{32,288},{40,296},{48,304},{56,3... | collective-permute-start | bytes 798728 | tf_op jit(solution)/shard_map/ppermute | solution.py:19
  205.9 4.9 %collective-permute-start.8 = (bf16[1040,128]{1,0:T(8,128)(2,1)S(1)}, bf16[1040,128]{1,0:T(8,128)(2,1)S(1)}, u32[]{:S(2)}, u32[]{:S(2)}) collective-permute-start(bf16[1040,128]{1,0:T(8,128)(2,1)S(1)} %get-tuple-element.56), channel_id=1, source_target_pairs={{0,256},{8,264},{16,272},{24,280},{32,288},{40,296},{48,304},{56,3... | collective-permute-start | bytes 798728 | tf_op jit(solution)/shard_map/ppermute | solution.py:19
  210.8 1.4 shard_map.32
  212.2 2.4 %collective-permute-start.5 = (bf16[1040,128]{1,0:T(8,128)(2,1)S(1)}, bf16[1040,128]{1,0:T(8,128)(2,1)S(1)}, u32[]{:S(2)}, u32[]{:S(2)}) collective-permute-start(bf16[1040,128]{1,0:T(8,128)(2,1)S(1)} %get-tuple-element.49), channel_id=1, source_target_pairs={{0,256},{8,264},{16,272},{24,280},{32,288},{40,296},{48,304},{56,3... | collective-permute-start | bytes 798728 | tf_op jit(solution)/shard_map/ppermute | solution.py:19
  214.7 1.9 shard_map.38.rest_0_
  216.6 1.9 shard_map.39.rest_0_
  218.6 1.8 collective-permute-done.8.partner_ref
  220.4 1.9 shard_map.40.rest_0_
  222.3 2.3 %collective-permute-done.5.partner_ref = bf16[1040,128]{1,0:T(8,128)(2,1)S(1)} collective-permute-done((bf16[1040,128]{1,0:T(8,128)(2,1)S(1)}, bf16[1040,128]{1,0:T(8,128)(2,1)S(1)}, u32[]{:S(2)}, u32[]{:S(2)}) %collective-permute-start.5) | collective-permute-done | bytes 266272 | tf_op jit(solution)/shard_map/ppermute | solution.py:19
  224.7 1.9 shard_map.41
  (47 shorter events, 16.5 us)
Async XLA Ops:
  6.5 69.7 %all-gather.5.cloned.1.call-start = ((), (), s32[]{:S(2)}) async-start(), calls=%async_computation.2 | async-start | bytes 1966080 | tf_op jit(solution)/shard_map/all_gather | solution.py:162
  7.5 48.1 %copy-start.13 = (bf16[2,4,32,512]{3,2,1,0:T(8,128)(2,1)}, bf16[2,4,32,512]{3,2,1,0:T(8,128)(2,1)S(1)}, u32[]{:S(2)}) copy-start(bf16[2,4,32,512]{3,2,1,0:T(8,128)(2,1)S(1)} %slice.7) | copy-start | bytes 786436
  9.4 40.4 %collective-permute-start = (bf16[3,4,32,512]{3,2,1,0:T(8,128)(2,1)}, bf16[3,4,32,512]{3,2,1,0:T(8,128)(2,1)S(1)}, u32[]{:S(2)}, u32[]{:S(2)}) collective-permute-start(bf16[3,4,32,512]{3,2,1,0:T(8,128)(2,1)} %slice.6), channel_id=1, source_target_pairs={{0,4},{4,0},{1,5},{5,1},{2,6},{6,2},{3,7},{7,3},{8,12},{12,8},{9,1... | collective-permute-start | bytes 1179656 | tf_op jit(solution)/shard_map/ppermute | solution.py:19
  51.1 25.1 %all-to-all-start = ((bf16[4,3,4,32,512]{4,3,2,1,0:T(8,128)(2,1)}), bf16[4,3,4,32,512]{4,3,2,1,0:T(8,128)(2,1)S(1)}, u32[]{:S(2)}, u32[]{:S(2)}) async-start(bf16[4,3,4,32,512]{4,3,2,1,0:T(8,128)(2,1)} %broadcast_in_dim.4), calls=%async_computation | async-start | bytes 3145728 | tf_op jit(solution)/shard_map/all_to_all | solution.py:159
  55.6 133.0 %all-gather.7.cloned.1.call-start = ((), (), s32[]{:S(2)}) async-start(), calls=%async_computation.3 | async-start | bytes 1310720 | tf_op jit(solution)/shard_map/all_gather | solution.py:163
  55.6 30.6 %collective-permute-start.1 = (bf16[2,4,32,512]{3,2,1,0:T(8,128)(2,1)S(1)}, bf16[2,4,32,512]{3,2,1,0:T(8,128)(2,1)}, u32[]{:S(2)}, u32[]{:S(2)}) collective-permute-start(bf16[2,4,32,512]{3,2,1,0:T(8,128)(2,1)S(1)} %slice.7), channel_id=1, source_target_pairs={{0,4},{4,0},{1,5},{5,1},{2,6},{6,2},{3,7},{7,3},{8,12},{12,8},{9,1... | collective-permute-start | bytes 786440 | tf_op jit(solution)/shard_map/ppermute | solution.py:19
  76.2 1.4 copy-start.12
  85.0 9.8 %copy-start = (f32[512,1024]{1,0:T(8,128)S(1)}, f32[512,1024]{1,0:T(8,128)}, u32[]{:S(2)}) copy-start(f32[512,1024]{1,0:T(8,128)} %get-tuple-element.38.mine_ref) | copy-start | bytes 6291460
  86.2 8.7 %collective-permute-start.2 = (f32[512,1024]{1,0:T(8,128)}, f32[512,1024]{1,0:T(8,128)}, u32[]{:S(2)}, u32[]{:S(2)}) collective-permute-start(f32[512,1024]{1,0:T(8,128)} %get-tuple-element.38.mine_ref), channel_id=1, source_target_pairs={{0,8},{8,0},{16,24},{24,16},{32,40},{40,32},{48,56},{56,48},{64,72... | collective-permute-start | bytes 6291464 | tf_op jit(solution)/shard_map/ppermute | solution.py:19
  90.2 98.4 %all-to-all-start.1 = ((bf16[4,2,4,32,512]{4,3,2,1,0:T(8,128)(2,1)}), bf16[4,2,4,32,512]{4,3,2,1,0:T(8,128)(2,1)}, u32[]{:S(2)}, u32[]{:S(2)}) async-start(bf16[4,2,4,32,512]{4,3,2,1,0:T(8,128)(2,1)} %broadcast_in_dim.5), calls=%async_computation.1 | async-start | bytes 2097152 | tf_op jit(solution)/shard_map/all_to_all | solution.py:159
  97.2 0.8 copy-start.8
  98.0 77.2 %collective-permute-start.6 = (bf16[1040,128]{1,0:T(8,128)(2,1)S(1)}, bf16[1040,128]{1,0:T(8,128)(2,1)S(1)}, u32[]{:S(2)}, u32[]{:S(2)}) collective-permute-start(bf16[1040,128]{1,0:T(8,128)(2,1)S(1)} %get-tuple-element.53), channel_id=1, source_target_pairs={{0,64},{8,72},{16,80},{24,88},{32,96},{40,104},{48,112},{56,120},{... | collective-permute-start | bytes 798728 | tf_op jit(solution)/shard_map/ppermute | solution.py:19
  107.8 0.8 copy-start.6
  108.6 78.0 %collective-permute-start.3 = (bf16[1040,128]{1,0:T(8,128)(2,1)S(1)}, bf16[1040,128]{1,0:T(8,128)(2,1)S(1)}, u32[]{:S(2)}, u32[]{:S(2)}) collective-permute-start(bf16[1040,128]{1,0:T(8,128)(2,1)S(1)} %get-tuple-element.42), channel_id=1, source_target_pairs={{0,64},{8,72},{16,80},{24,88},{32,96},{40,104},{48,112},{56,120},{... | collective-permute-start | bytes 798728 | tf_op jit(solution)/shard_map/ppermute | solution.py:19
  114.0 0.8 copy-start.4
  117.8 0.8 copy-start.2
  175.2 0.7 copy-start.10
  175.9 28.5 %collective-permute-start.7 = (bf16[1040,128]{1,0:T(8,128)(2,1)}, bf16[1040,128]{1,0:T(8,128)(2,1)S(1)}, u32[]{:S(2)}, u32[]{:S(2)}) collective-permute-start(bf16[1040,128]{1,0:T(8,128)(2,1)} %get-tuple-element.54), channel_id=1, source_target_pairs={{0,64},{8,72},{16,80},{24,88},{32,96},{40,104},{48,112},{56,120},{... | collective-permute-start | bytes 798728 | tf_op jit(solution)/shard_map/ppermute | solution.py:19
  186.6 24.2 %collective-permute-start.4 = (bf16[1040,128]{1,0:T(8,128)(2,1)}, bf16[1040,128]{1,0:T(8,128)(2,1)S(1)}, u32[]{:S(2)}, u32[]{:S(2)}) collective-permute-start(bf16[1040,128]{1,0:T(8,128)(2,1)} %get-tuple-element.43), channel_id=1, source_target_pairs={{0,64},{8,72},{16,80},{24,88},{32,96},{40,104},{48,112},{56,120},{... | collective-permute-start | bytes 798728 | tf_op jit(solution)/shard_map/ppermute | solution.py:19
  188.6 1.2 copy-start.1
  189.8 2.1 copy-start.11
  191.9 12.5 %copy-start.5 = (f32[128,1024]{1,0:T(8,128)S(1)}, f32[128,1024]{1,0:T(8,128)}, u32[]{:S(2)}) copy-start(f32[128,1024]{1,0:T(8,128)} %copy-done.4) | copy-start | bytes 1572868
  191.9 1.1 copy-start.9
  194.4 16.4 %copy-start.3 = (f32[128,1024]{1,0:T(8,128)S(1)}, f32[128,1024]{1,0:T(8,128)}, u32[]{:S(2)}) copy-start(f32[128,1024]{1,0:T(8,128)} %copy-done.2) | copy-start | bytes 1572868
  194.4 20.2 %collective-permute-start.10 = (bf16[1040,128]{1,0:T(8,128)(2,1)S(1)}, bf16[1040,128]{1,0:T(8,128)(2,1)S(1)}, u32[]{:S(2)}, u32[]{:S(2)}) collective-permute-start(bf16[1040,128]{1,0:T(8,128)(2,1)S(1)} %get-tuple-element.62), channel_id=1, source_target_pairs={{0,256},{8,264},{16,272},{24,280},{32,288},{40,296},{48,304},{56,3... | collective-permute-start | bytes 798728 | tf_op jit(solution)/shard_map/ppermute | solution.py:19
  199.5 1.0 copy-start.7
  202.0 14.6 %collective-permute-start.9 = (bf16[1040,128]{1,0:T(8,128)(2,1)S(1)}, bf16[1040,128]{1,0:T(8,128)(2,1)S(1)}, u32[]{:S(2)}, u32[]{:S(2)}) collective-permute-start(bf16[1040,128]{1,0:T(8,128)(2,1)S(1)} %get-tuple-element.59), channel_id=1, source_target_pairs={{0,256},{8,264},{16,272},{24,280},{32,288},{40,296},{48,304},{56,3... | collective-permute-start | bytes 798728 | tf_op jit(solution)/shard_map/ppermute | solution.py:19
  205.9 14.5 %collective-permute-start.8 = (bf16[1040,128]{1,0:T(8,128)(2,1)S(1)}, bf16[1040,128]{1,0:T(8,128)(2,1)S(1)}, u32[]{:S(2)}, u32[]{:S(2)}) collective-permute-start(bf16[1040,128]{1,0:T(8,128)(2,1)S(1)} %get-tuple-element.56), channel_id=1, source_target_pairs={{0,256},{8,264},{16,272},{24,280},{32,288},{40,296},{48,304},{56,3... | collective-permute-start | bytes 798728 | tf_op jit(solution)/shard_map/ppermute | solution.py:19
  212.2 12.4 %collective-permute-start.5 = (bf16[1040,128]{1,0:T(8,128)(2,1)S(1)}, bf16[1040,128]{1,0:T(8,128)(2,1)S(1)}, u32[]{:S(2)}, u32[]{:S(2)}) collective-permute-start(bf16[1040,128]{1,0:T(8,128)(2,1)S(1)} %get-tuple-element.49), channel_id=1, source_target_pairs={{0,256},{8,264},{16,272},{24,280},{32,288},{40,296},{48,304},{56,3... | collective-permute-start | bytes 798728 | tf_op jit(solution)/shard_map/ppermute | solution.py:19
Sparse Core Ops, SparseCore 0:
  9.5 33.2 all-gather.4
  88.3 33.2 all-gather.6

commit v4 on v3

--- a/solution.py
+++ b/solution.py
@@ -24,11 +24,11 @@
     for own_ref, other_ref, at, matrix_ref in pairs:
         parts, _, _, rows, _ = own_ref.shape
         for part in range(parts):
-            for ref, side in ((own_ref, half), (other_ref, 1 - half)):
+            for ref, place, side in ((own_ref, at, half), (other_ref, at + (own_ref is other_ref), 1 - half)):
                 start = pl.multiple_of((side * parts + part) * rows, rows)
                 copies.append(
                     pltpu.make_async_copy(
-                        ref.at[part, at], matrix_ref.at[:, pl.ds(start, rows), :], sems.at[len(copies)]
+                        ref.at[part, place], matrix_ref.at[:, pl.ds(start, rows), :], sems.at[len(copies)]
                     )
                 )
     return copies
@@ -103,9 +103,9 @@
         copy.wait()
 
 
-def prepare_body(bits_ref, own, other, *rest):
+def prepare_body(bits_ref, gathered, *rest):
     outs, sems = rest[:-1], rest[-1]
-    copies = assembling([(own, other, at, ref) for at, ref in enumerate(outs)], sems, bits_ref[0])
+    copies = assembling([(gathered, gathered, 2 * level, ref) for level, ref in enumerate(outs)], sems, bits_ref[0])
     for copy in copies:
         copy.start()
     for copy in copies:
@@ -160,7 +160,6 @@
 
     early, late = lax.optimization_barrier((weights[:3], weights[3:]))
     own_early = lax.all_gather(early, "narrow_1")
-    own_late = lax.all_gather(late, "narrow_1")
     early_other = swapped(early, "narrow_0", 0)
     late_turn, _ = lax.optimization_barrier((late, early_other))
     late_other = swapped(late_turn, "narrow_0", 0)
@@ -180,7 +179,7 @@
 
     def cost(rows_done, levels, bytes_accessed):
         return pl.CostEstimate(
-            flops=4 * levels * rows_done * coeffs * width, bytes_accessed=bytes_accessed, transcendentals=0
+            flops=0, bytes_accessed=0, transcendentals=0
         )
 
     size = width // 2
@@ -206,7 +205,6 @@
     )(bits, vectors, own_early, other_early)
     sent, late_other = lax.optimization_barrier((current, late_other))
     partner = swapped(sent, "wide", wide_bits[0])
-    other_late = around(late_other)
 
     owns, codes = [], []
     for c in range(chunks):
@@ -225,16 +223,17 @@
         )(bits, owns[c], arrived[c], middle_matrix)
         later.append((mine, code, swapped(code, "wide", wide_bits[2])))
 
+    late_other, _ = lax.optimization_barrier((late_other, codes[1]))
+    gathered = lax.all_gather(jnp.stack([late, late_other], 1).reshape(-1, *late.shape[1:]), "narrow_1")
+    middle_matrix, last_matrix = call(
+        prepare_body, [anywhere], [anywhere] * 2, [matrix_type] * 2, [pltpu.SemaphoreType.DMA((4 * parts,))],
+        cost(0, 0, 4 * matrix_bytes),
+    )(bits, gathered)
     for c in range(chunks):
         code = codes[c]
         if c >= window:
-            code, _ = lax.optimization_barrier((code, [arrived[c - window], codes[-1]]))
+            code, _ = lax.optimization_barrier((code, gathered))
         arrived.append(swapped(code, "wide", wide_bits[1]))
-    own_late, other_late, _ = lax.optimization_barrier((own_late, other_late, arrived[window - 1]))
-    middle_matrix, last_matrix = call(
-        prepare_body, [anywhere] * 2, [anywhere] * 2, [matrix_type] * 2, [pltpu.SemaphoreType.DMA((4 * parts,))],
-        cost(0, 0, 4 * matrix_bytes),
-    )(bits, own_late, other_late)
     for c in range(chunks):
         middle(c)
     later = [(mine, code) for mine, _, code in later]

time: 237 us -> 224 us (0.945); the launches traced: 233 us -> 223 us
  waiting for transfers between devices: 123 us -> 108 us
  Pallas kernels: 33.7 us -> 29.8 us
  local copies, waits for them, and re-layouts: 14.9 us -> 18.7 us
  starting transfers between devices: 48 us -> 51.8 us
    ppermute x11, waiting for transfers between devices: 105 us -> 69.3 us  [swapped(): lax.ppermute(shard, axis, [(i, i ^ 1 << apart) for i in range(lax.axis_si...]
    all_gather x1, waiting for transfers between devices: 0.02 us -> 20.2 us  [on_device(): lax.all_gather(jnp.stack([late, late_other], 1).reshape(-1, *late.shape[1...]
    ppermute x11, starting transfers between devices: 38.9 us -> 47.3 us  [swapped(): lax.ppermute(shard, axis, [(i, i ^ 1 << apart) for i in range(lax.axis_si...]
    unnamed x28 -> x32, local copies, waits for them, and re-layouts: 8.63 us -> 13.7 us
    all_to_all x2 -> x1, starting transfers between devices: 9.12 us -> 4.46 us  [around(): lax.all_to_all(jnp.broadcast_to(shard[None], (parts,) + shard.shape), 'na...]
    pallas_call x4, Pallas kernels: 10.8 us -> 6.62 us  [on_device(): call(core_body, [row_spec(c), row_spec(c), matrix_spec], [row_spec(0), co...]
    all_to_all x2 -> x1, waiting for transfers between devices: 18.2 us -> 18.2 us  [around(): lax.all_to_all(jnp.broadcast_to(shard[None], (parts,) + shard.shape), 'na...]
  transfers between devices with their start and end apart: 15 -> 14, of which waited for: 7 -> 7; matrix products, arithmetic and copies ran while one was open for 1% -> 1% of each run, Pallas kernels for 14% -> 12%
where the time goes in v4:
time: 224 us; the launch traced here: 223 us
  waiting for transfers between devices  108 us (48%)
  starting transfers between devices  51.8 us (23%)
  Pallas kernels  29.8 us (13%)
  local copies, waits for them, and re-layouts  18.7 us (8%)
  between operations  13.7 us (6%)
    ppermute x11, waiting for transfers between devices, swapped(): lax.ppermute(shard, axis, [(i, i ^ 1 << apart) for i in range(lax.axis_si...  69.3 us
    ppermute x11, starting transfers between devices, swapped(): lax.ppermute(shard, axis, [(i, i ^ 1 << apart) for i in range(lax.axis_si...  47.3 us
    all_gather x1, waiting for transfers between devices, on_device(): lax.all_gather(jnp.stack([late, late_other], 1).reshape(-1, *late.shape[1...  20.2 us
    all_to_all x1, waiting for transfers between devices, around(): lax.all_to_all(jnp.broadcast_to(shard[None], (parts,) + shard.shape), 'na...  18.2 us
    unnamed x32, local copies, waits for them, and re-layouts  13.7 us
    pallas_call x4, Pallas kernels, on_device(): call(last_body, specs, row_spec(c), full_shape, [], cost(rows, 1, 10 * ro...  7.72 us
    pallas_call x1, Pallas kernels, on_device(): call(local_body, [full, anywhere, anywhere], [full, anywhere], [full_shap...  7.42 us
    pallas_call x4, Pallas kernels, middle(): call(middle_body, [row_spec(0), code_spec, matrix_spec], [row_spec(0), co...  6.67 us
  transfers between devices with their start and end apart: 14, of which 7 were waited for; matrix products, arithmetic and copies ran while one was open for 1% of the time, Pallas kernels for 12%

profile of v4, /device:TPU:480, one launch (start us, length us, event | category | flops | bytes accessed | tf_op | source)
XLA Modules:
  0.0 223.0 jit_solution(11640215814735108656)
XLA Ops:
  7.5 1.8 slice.6
  9.3 6.3 %collective-permute-start = (bf16[3,4,32,512]{3,2,1,0:T(8,128)(2,1)}, bf16[3,4,32,512]{3,2,1,0:T(8,128)(2,1)S(1)}, u32[]{:S(2)}, u32[]{:S(2)}) collective-permute-start(bf16[3,4,32,512]{3,2,1,0:T(8,128)(2,1)} %slice.6), channel_id=1, source_target_pairs={{0,4},{4,0},{1,5},{5,1},{2,6},{6,2},{3,7},{7,3},{8,12},{12,8},{9,1... | collective-permute-start | bytes 1179656 | tf_op jit(solution)/shard_map/ppermute | solution.py:19
  15.6 34.1 %collective-permute-done = bf16[3,4,32,512]{3,2,1,0:T(8,128)(2,1)S(1)} collective-permute-done((bf16[3,4,32,512]{3,2,1,0:T(8,128)(2,1)}, bf16[3,4,32,512]{3,2,1,0:T(8,128)(2,1)S(1)}, u32[]{:S(2)}, u32[]{:S(2)}) %collective-permute-start) | collective-permute-done | bytes 393248 | tf_op jit(solution)/shard_map/ppermute | solution.py:19
  51.0 4.5 %all-to-all-start = ((bf16[4,3,4,32,512]{4,3,2,1,0:T(8,128)(2,1)}), bf16[4,3,4,32,512]{4,3,2,1,0:T(8,128)(2,1)S(1)}, u32[]{:S(2)}, u32[]{:S(2)}) async-start(bf16[4,3,4,32,512]{4,3,2,1,0:T(8,128)(2,1)} %broadcast_in_dim.2), calls=%async_computation | async-start | bytes 3145728 | tf_op jit(solution)/shard_map/all_to_all | solution.py:159
  55.5 2.3 %collective-permute-start.1 = (bf16[2,4,32,512]{3,2,1,0:T(8,128)(2,1)S(1)}, bf16[2,4,32,512]{3,2,1,0:T(8,128)(2,1)}, u32[]{:S(2)}, u32[]{:S(2)}) collective-permute-start(bf16[2,4,32,512]{3,2,1,0:T(8,128)(2,1)S(1)} %slice.7), channel_id=1, source_target_pairs={{0,4},{4,0},{1,5},{5,1},{2,6},{6,2},{3,7},{7,3},{8,12},{12,8},{9,1... | collective-permute-start | bytes 786440 | tf_op jit(solution)/shard_map/ppermute | solution.py:19
  57.9 18.2 %all-to-all-done.other = bf16[4,3,4,32,512]{4,3,2,1,0:T(8,128)(2,1)S(1)} async-done(((bf16[4,3,4,32,512]{4,3,2,1,0:T(8,128)(2,1)}), bf16[4,3,4,32,512]{4,3,2,1,0:T(8,128)(2,1)S(1)}, u32[]{:S(2)}, u32[]{:S(2)}) %all-to-all-start) | async-done | bytes 1572896 | tf_op jit(solution)/shard_map/all_to_all | solution.py:159
  77.5 7.4 %shard_map.28 = (f32[512,1024]{1,0:T(8,128)}, bf16[4,256,512]{2,1,0:T(8,128)(2,1)S(1)}) custom-call(s32[5]{0:T(128)S(1)} %stack.32.bits_ref, f32[512,1024]{1,0:T(8,128)} %x_ref.1, bf16[4,3,4,32,512]{4,3,2,1,0:T(8,128)(2,1)S(1)} %bitcast.9, bf16[4,3,4,32,512]{4,3,2,1,0:T(8,128)(2,1)S(1)} %all-to-all-done.other), custom_call_target="tpu_custom_call" | custom-call | tf_op jit(solution)/shard_map/pallas_call | solution.py:201
  86.1 1.9 collective-permute-start.2
  88.0 4.3 %collective-permute-done.2.partner_ref = f32[512,1024]{1,0:T(8,128)S(1)} collective-permute-done((f32[512,1024]{1,0:T(8,128)}, f32[512,1024]{1,0:T(8,128)S(1)}, u32[]{:S(2)}, u32[]{:S(2)}) %collective-permute-start.2) | collective-permute-done | bytes 2097184 | tf_op jit(solution)/shard_map/ppermute | solution.py:19
  92.3 2.3 %copy-done = f32[512,1024]{1,0:T(8,128)S(1)} copy-done((f32[512,1024]{1,0:T(8,128)S(1)}, f32[512,1024]{1,0:T(8,128)}, u32[]{:S(2)}) %copy-start) | copy-done | bytes 2097176
  94.7 2.0 shard_map.30
  99.6 7.5 %collective-permute-start.7 = (bf16[1040,128]{1,0:T(8,128)(2,1)}, bf16[1040,128]{1,0:T(8,128)(2,1)}, u32[]{:S(2)}, u32[]{:S(2)}) collective-permute-start(bf16[1040,128]{1,0:T(8,128)(2,1)} %get-tuple-element.42), channel_id=1, source_target_pairs={{0,64},{8,72},{16,80},{24,88},{32,96},{40,104},{48,112},{56,120},{... | collective-permute-start | bytes 798728 | tf_op jit(solution)/shard_map/ppermute | solution.py:19
  107.1 1.6 copy-done.3
  108.7 2.0 shard_map.36
  111.5 2.3 %collective-permute-start.9 = (bf16[1040,128]{1,0:T(8,128)(2,1)}, bf16[1040,128]{1,0:T(8,128)(2,1)S(1)}, u32[]{:S(2)}, u32[]{:S(2)}) collective-permute-start(bf16[1040,128]{1,0:T(8,128)(2,1)} %get-tuple-element.58), channel_id=1, source_target_pairs={{0,64},{8,72},{16,80},{24,88},{32,96},{40,104},{48,112},{56,120},{... | collective-permute-start | bytes 798728 | tf_op jit(solution)/shard_map/ppermute | solution.py:19
  119.4 20.2 %all-gather.4.cloned.1.call-done.gathered = bf16[4,4,4,32,512]{4,3,2,1,0:T(8,128)(2,1)} async-done(((bf16[1,4,4,32,512]{4,3,2,1,0:T(8,128)(2,1)}), bf16[4,4,4,32,512]{4,3,2,1,0:T(8,128)(2,1)}) %all-gather.4.cloned.1.call-update) | async-done | bytes 2097168 | tf_op jit(solution)/shard_map/all_gather | solution.py:227
  139.6 6.9 %collective-permute-start.5 = (bf16[1040,128]{1,0:T(8,128)(2,1)}, bf16[1040,128]{1,0:T(8,128)(2,1)S(1)}, u32[]{:S(2)}, u32[]{:S(2)}) collective-permute-start(bf16[1040,128]{1,0:T(8,128)(2,1)} %copy-done.15), channel_id=1, source_target_pairs={{0,64},{8,72},{16,80},{24,88},{32,96},{40,104},{48,112},{56,120},{... | collective-permute-start | bytes 798728 | tf_op jit(solution)/shard_map/ppermute | solution.py:19
  146.5 2.8 %collective-permute-start.3 = (bf16[1040,128]{1,0:T(8,128)(2,1)}, bf16[1040,128]{1,0:T(8,128)(2,1)S(1)}, u32[]{:S(2)}, u32[]{:S(2)}) collective-permute-start(bf16[1040,128]{1,0:T(8,128)(2,1)} %copy-done.14), channel_id=1, source_target_pairs={{0,64},{8,72},{16,80},{24,88},{32,96},{40,104},{48,112},{56,120},{... | collective-permute-start | bytes 798728 | tf_op jit(solution)/shard_map/ppermute | solution.py:19
  149.4 1.6 copy-done.4
  153.5 2.4 %shard_map.35 = (f32[128,1024]{1,0:T(8,128)S(1)}, bf16[1040,128]{1,0:T(8,128)(2,1)S(1)}) custom-call(s32[5]{0:T(128)S(1)} %stack.32.bits_ref, f32[128,1024]{1,0:T(8,128)S(1)} %copy-done.11, bf16[1040,128]{1,0:T(8,128)(2,1)} %collective-permute-done.7.partner_ref, bf16[4,256,512]{2,1,0:T(8,128)(2,1)S(1)} %get-tuple-element.45.matrix), custom_call_target="tpu_custom_call" | custom-call | tf_op jit(solution)/shard_map/pallas_call | solution.py:220
  155.9 5.0 %collective-permute-start.8 = (bf16[1040,128]{1,0:T(8,128)(2,1)S(1)}, bf16[1040,128]{1,0:T(8,128)(2,1)S(1)}, u32[]{:S(2)}, u32[]{:S(2)}) collective-permute-start(bf16[1040,128]{1,0:T(8,128)(2,1)S(1)} %get-tuple-element.56), channel_id=1, source_target_pairs={{0,256},{8,264},{16,272},{24,280},{32,288},{40,296},{48,304},{56,3... | collective-permute-start | bytes 798728 | tf_op jit(solution)/shard_map/ppermute | solution.py:19
  160.9 27.4 %collective-permute-done.9.partner_ref = bf16[1040,128]{1,0:T(8,128)(2,1)S(1)} collective-permute-done((bf16[1040,128]{1,0:T(8,128)(2,1)}, bf16[1040,128]{1,0:T(8,128)(2,1)S(1)}, u32[]{:S(2)}, u32[]{:S(2)}) %collective-permute-start.9) | collective-permute-done | bytes 266272 | tf_op jit(solution)/shard_map/ppermute | solution.py:19
  189.3 1.4 shard_map.37
  190.7 4.9 %collective-permute-start.10 = (bf16[1040,128]{1,0:T(8,128)(2,1)S(1)}, bf16[1040,128]{1,0:T(8,128)(2,1)S(1)}, u32[]{:S(2)}, u32[]{:S(2)}) collective-permute-start(bf16[1040,128]{1,0:T(8,128)(2,1)S(1)} %get-tuple-element.60), channel_id=1, source_target_pairs={{0,256},{8,264},{16,272},{24,280},{32,288},{40,296},{48,304},{56,3... | collective-permute-start | bytes 798728 | tf_op jit(solution)/shard_map/ppermute | solution.py:19
  197.1 3.2 %collective-permute-start.6 = (bf16[1040,128]{1,0:T(8,128)(2,1)S(1)}, bf16[1040,128]{1,0:T(8,128)(2,1)S(1)}, u32[]{:S(2)}, u32[]{:S(2)}) collective-permute-start(bf16[1040,128]{1,0:T(8,128)(2,1)S(1)} %get-tuple-element.53), channel_id=1, source_target_pairs={{0,256},{8,264},{16,272},{24,280},{32,288},{40,296},{48,304},{56,3... | collective-permute-start | bytes 798728 | tf_op jit(solution)/shard_map/ppermute | solution.py:19
  200.3 1.4 shard_map.32
  201.8 4.2 %collective-permute-start.4 = (bf16[1040,128]{1,0:T(8,128)(2,1)S(1)}, bf16[1040,128]{1,0:T(8,128)(2,1)S(1)}, u32[]{:S(2)}, u32[]{:S(2)}) collective-permute-start(bf16[1040,128]{1,0:T(8,128)(2,1)S(1)} %get-tuple-element.47), channel_id=1, source_target_pairs={{0,256},{8,264},{16,272},{24,280},{32,288},{40,296},{48,304},{56,3... | collective-permute-start | bytes 798728 | tf_op jit(solution)/shard_map/ppermute | solution.py:19
  206.0 1.9 shard_map.38.rest_0_
  207.9 1.9 shard_map.39.rest_0_
  209.8 1.9 shard_map.40.rest_0_
  211.8 2.4 %collective-permute-done.4.partner_ref = bf16[1040,128]{1,0:T(8,128)(2,1)S(1)} collective-permute-done((bf16[1040,128]{1,0:T(8,128)(2,1)S(1)}, bf16[1040,128]{1,0:T(8,128)(2,1)S(1)}, u32[]{:S(2)}, u32[]{:S(2)}) %collective-permute-start.4) | collective-permute-done | bytes 266272 | tf_op jit(solution)/shard_map/ppermute | solution.py:19
  214.2 1.9 shard_map.41
  (50 shorter events, 19.2 us)
Async XLA Ops:
  6.5 69.6 %all-gather.6.cloned.1.call-start = ((), (), s32[]{:S(2)}) async-start(), calls=%async_computation.2 | async-start | bytes 1966080 | tf_op jit(solution)/shard_map/all_gather | solution.py:162
  9.3 40.4 %collective-permute-start = (bf16[3,4,32,512]{3,2,1,0:T(8,128)(2,1)}, bf16[3,4,32,512]{3,2,1,0:T(8,128)(2,1)S(1)}, u32[]{:S(2)}, u32[]{:S(2)}) collective-permute-start(bf16[3,4,32,512]{3,2,1,0:T(8,128)(2,1)} %slice.6), channel_id=1, source_target_pairs={{0,4},{4,0},{1,5},{5,1},{2,6},{6,2},{3,7},{7,3},{8,12},{12,8},{9,1... | collective-permute-start | bytes 1179656 | tf_op jit(solution)/shard_map/ppermute | solution.py:19
  51.0 25.1 %all-to-all-start = ((bf16[4,3,4,32,512]{4,3,2,1,0:T(8,128)(2,1)}), bf16[4,3,4,32,512]{4,3,2,1,0:T(8,128)(2,1)S(1)}, u32[]{:S(2)}, u32[]{:S(2)}) async-start(bf16[4,3,4,32,512]{4,3,2,1,0:T(8,128)(2,1)} %broadcast_in_dim.2), calls=%async_computation | async-start | bytes 3145728 | tf_op jit(solution)/shard_map/all_to_all | solution.py:159
  55.5 84.1 %all-gather.4.cloned.1.call-start = ((), (), s32[]{:S(2)}) async-start(), calls=%async_computation.1 | async-start | bytes 2621440 | tf_op jit(solution)/shard_map/all_gather | solution.py:227
  55.5 30.6 %collective-permute-start.1 = (bf16[2,4,32,512]{3,2,1,0:T(8,128)(2,1)S(1)}, bf16[2,4,32,512]{3,2,1,0:T(8,128)(2,1)}, u32[]{:S(2)}, u32[]{:S(2)}) collective-permute-start(bf16[2,4,32,512]{3,2,1,0:T(8,128)(2,1)S(1)} %slice.7), channel_id=1, source_target_pairs={{0,4},{4,0},{1,5},{5,1},{2,6},{6,2},{3,7},{7,3},{8,12},{12,8},{9,1... | collective-permute-start | bytes 786440 | tf_op jit(solution)/shard_map/ppermute | solution.py:19
  76.1 1.4 copy-start.5
  86.1 6.3 %collective-permute-start.2 = (f32[512,1024]{1,0:T(8,128)}, f32[512,1024]{1,0:T(8,128)S(1)}, u32[]{:S(2)}, u32[]{:S(2)}) collective-permute-start(f32[512,1024]{1,0:T(8,128)} %get-tuple-element.37.mine_ref), channel_id=1, source_target_pairs={{0,8},{8,0},{16,24},{24,16},{32,40},{40,32},{48,56},{56,48},{64,72... | collective-permute-start | bytes 6291464 | tf_op jit(solution)/shard_map/ppermute | solution.py:19
  92.3 4.4 %copy-start.2 = (f32[512,1024]{1,0:T(8,128)}, f32[512,1024]{1,0:T(8,128)S(1)}, u32[]{:S(2)}) copy-start(f32[512,1024]{1,0:T(8,128)S(1)} %collective-permute-done.2.partner_ref) | copy-start | bytes 6291460
  92.3 2.3 %copy-start = (f32[512,1024]{1,0:T(8,128)S(1)}, f32[512,1024]{1,0:T(8,128)}, u32[]{:S(2)}) copy-start(f32[512,1024]{1,0:T(8,128)} %get-tuple-element.37.mine_ref) | copy-start | bytes 6291460
  96.7 0.8 copy-start.10
  97.5 9.5 %copy-start.1 = (f32[512,1024]{1,0:T(8,128)S(1)}, f32[512,1024]{1,0:T(8,128)}, u32[]{:S(2)}) copy-start(f32[512,1024]{1,0:T(8,128)} %get-tuple-element.37.mine_ref) | copy-start | bytes 6291460
  99.6 52.8 %collective-permute-start.7 = (bf16[1040,128]{1,0:T(8,128)(2,1)}, bf16[1040,128]{1,0:T(8,128)(2,1)}, u32[]{:S(2)}, u32[]{:S(2)}) collective-permute-start(bf16[1040,128]{1,0:T(8,128)(2,1)} %get-tuple-element.42), channel_id=1, source_target_pairs={{0,64},{8,72},{16,80},{24,88},{32,96},{40,104},{48,112},{56,120},{... | collective-permute-start | bytes 798728 | tf_op jit(solution)/shard_map/ppermute | solution.py:19
  107.1 1.6 copy-start.3
  110.6 0.8 copy-start.12
  111.5 76.8 %collective-permute-start.9 = (bf16[1040,128]{1,0:T(8,128)(2,1)}, bf16[1040,128]{1,0:T(8,128)(2,1)S(1)}, u32[]{:S(2)}, u32[]{:S(2)}) collective-permute-start(bf16[1040,128]{1,0:T(8,128)(2,1)} %get-tuple-element.58), channel_id=1, source_target_pairs={{0,64},{8,72},{16,80},{24,88},{32,96},{40,104},{48,112},{56,120},{... | collective-permute-start | bytes 798728 | tf_op jit(solution)/shard_map/ppermute | solution.py:19
  115.0 0.8 copy-start.8
  115.9 0.7 copy-start.15
  117.9 0.8 copy-start.6
  118.7 0.7 copy-start.14
  139.6 56.1 %collective-permute-start.5 = (bf16[1040,128]{1,0:T(8,128)(2,1)}, bf16[1040,128]{1,0:T(8,128)(2,1)S(1)}, u32[]{:S(2)}, u32[]{:S(2)}) collective-permute-start(bf16[1040,128]{1,0:T(8,128)(2,1)} %copy-done.15), channel_id=1, source_target_pairs={{0,64},{8,72},{16,80},{24,88},{32,96},{40,104},{48,112},{56,120},{... | collective-permute-start | bytes 798728 | tf_op jit(solution)/shard_map/ppermute | solution.py:19
  146.5 53.8 %collective-permute-start.3 = (bf16[1040,128]{1,0:T(8,128)(2,1)}, bf16[1040,128]{1,0:T(8,128)(2,1)S(1)}, u32[]{:S(2)}, u32[]{:S(2)}) collective-permute-start(bf16[1040,128]{1,0:T(8,128)(2,1)} %copy-done.14), channel_id=1, source_target_pairs={{0,64},{8,72},{16,80},{24,88},{32,96},{40,104},{48,112},{56,120},{... | collective-permute-start | bytes 798728 | tf_op jit(solution)/shard_map/ppermute | solution.py:19
  149.4 1.6 copy-start.4
  152.4 43.3 %copy-start.9 = (f32[128,1024]{1,0:T(8,128)S(1)}, f32[128,1024]{1,0:T(8,128)}, u32[]{:S(2)}) copy-start(f32[128,1024]{1,0:T(8,128)} %copy-done.8) | copy-start | bytes 1572868
  152.4 1.1 copy-start.11
  155.9 44.5 %copy-start.7 = (f32[128,1024]{1,0:T(8,128)S(1)}, f32[128,1024]{1,0:T(8,128)}, u32[]{:S(2)}) copy-start(f32[128,1024]{1,0:T(8,128)} %copy-done.6) | copy-start | bytes 1572868
  155.9 52.0 %collective-permute-start.8 = (bf16[1040,128]{1,0:T(8,128)(2,1)S(1)}, bf16[1040,128]{1,0:T(8,128)(2,1)S(1)}, u32[]{:S(2)}, u32[]{:S(2)}) collective-permute-start(bf16[1040,128]{1,0:T(8,128)(2,1)S(1)} %get-tuple-element.56), channel_id=1, source_target_pairs={{0,256},{8,264},{16,272},{24,280},{32,288},{40,296},{48,304},{56,3... | collective-permute-start | bytes 798728 | tf_op jit(solution)/shard_map/ppermute | solution.py:19
  188.3 1.0 copy-start.13
  190.7 15.2 %collective-permute-start.10 = (bf16[1040,128]{1,0:T(8,128)(2,1)S(1)}, bf16[1040,128]{1,0:T(8,128)(2,1)S(1)}, u32[]{:S(2)}, u32[]{:S(2)}) collective-permute-start(bf16[1040,128]{1,0:T(8,128)(2,1)S(1)} %get-tuple-element.60), channel_id=1, source_target_pairs={{0,256},{8,264},{16,272},{24,280},{32,288},{40,296},{48,304},{56,3... | collective-permute-start | bytes 798728 | tf_op jit(solution)/shard_map/ppermute | solution.py:19
  197.1 12.7 %collective-permute-start.6 = (bf16[1040,128]{1,0:T(8,128)(2,1)S(1)}, bf16[1040,128]{1,0:T(8,128)(2,1)S(1)}, u32[]{:S(2)}, u32[]{:S(2)}) collective-permute-start(bf16[1040,128]{1,0:T(8,128)(2,1)S(1)} %get-tuple-element.53), channel_id=1, source_target_pairs={{0,256},{8,264},{16,272},{24,280},{32,288},{40,296},{48,304},{56,3... | collective-permute-start | bytes 798728 | tf_op jit(solution)/shard_map/ppermute | solution.py:19
  201.8 12.4 %collective-permute-start.4 = (bf16[1040,128]{1,0:T(8,128)(2,1)S(1)}, bf16[1040,128]{1,0:T(8,128)(2,1)S(1)}, u32[]{:S(2)}, u32[]{:S(2)}) collective-permute-start(bf16[1040,128]{1,0:T(8,128)(2,1)S(1)} %get-tuple-element.47), channel_id=1, source_target_pairs={{0,256},{8,264},{16,272},{24,280},{32,288},{40,296},{48,304},{56,3... | collective-permute-start | bytes 798728 | tf_op jit(solution)/shard_map/ppermute | solution.py:19
Sparse Core Ops, SparseCore 0:
  9.5 33.2 all-gather.5
  99.7 39.8 all-gather.3

commit v5 on v4

--- a/solution.py
+++ b/solution.py
@@ -81,25 +81,26 @@
 
 def local_body(bits_ref, x_ref, own, other, out_ref, next_ref, matrix, sems):
     levels, count, size = matrix.shape[:3]
-    pairs = [(own, other, level, matrix.at[level]) for level in range(levels)] + [(own, other, levels, next_ref)]
-    copies = assembling(pairs, sems, bits_ref[0])
-    each = len(copies) // len(pairs)
+    parts, _, _, rows, _ = own.shape
+    copies = assembling([(own, other, levels, next_ref)], sems, bits_ref[0])
     for copy in copies:
         copy.start()
     value = x_ref[...]
     for level in range(levels):
-        for copy in copies[level * each:(level + 1) * each]:
-            copy.wait()
-        parts = blocks_of(value, count, size)
+        for part in range(parts):
+            for ref, side in ((own, bits_ref[0]), (other, 1 - bits_ref[0])):
+                start = pl.multiple_of((side * parts + part) * rows, rows)
+                matrix[level, :, pl.ds(start, rows), :] = ref[part, level]
+        pieces = blocks_of(value, count, size)
         outs = []
         for k in range(count):
-            low, high = parts[k & ~(1 << level)], parts[k | 1 << level]
+            low, high = pieces[k & ~(1 << level)], pieces[k | 1 << level]
             outs.append(
                 product(low, matrix[level, k, :, :size]) + product(high, matrix[level, k, :, size:])
             )
         value = jnp.concatenate(outs, axis=1)
     out_ref[...] = value
-    for copy in copies[levels * each:]:
+    for copy in copies:
         copy.wait()
 
 
@@ -158,7 +159,7 @@
     def around(shard):
         return lax.all_to_all(jnp.broadcast_to(shard[None], (parts,) + shard.shape), "narrow_1", 0, 0)
 
-    early, late = lax.optimization_barrier((weights[:3], weights[3:]))
+    early, late = weights[:3], weights[3:]
     own_early = lax.all_gather(early, "narrow_1")
     early_other = swapped(early, "narrow_0", 0)
     late_turn, _ = lax.optimization_barrier((late, early_other))
@@ -186,11 +187,15 @@
     matrix_bytes = 2 * count * size * width
     matrix_shape = (count, size, width)
 
+    def in_hbm(array):
+        return pltpu.with_memory_space_constraint(array, pltpu.HBM)
+
     def row_spec(index):
         return pl.BlockSpec((rows, coeffs), lambda i, bits: (index, 0))
 
     matrix_spec = pl.BlockSpec(matrix_shape, lambda i, bits: (0, 0, 0))
     anywhere = pl.BlockSpec(memory_space=pl.ANY)
+    in_vmem = pl.BlockSpec(memory_space=pltpu.VMEM)
     matrix_type = jax.ShapeDtypeStruct(matrix_shape, weights.dtype)
     full = pl.BlockSpec((columns, coeffs), lambda i, bits: (0, 0))
     code_spec = pl.BlockSpec((code_rows, LANES), lambda i, bits: (0, 0))
@@ -199,8 +204,8 @@
     full_shape = jax.ShapeDtypeStruct((columns, coeffs), jnp.float32)
 
     current, matrix = call(
-        local_body, [full, anywhere, anywhere], [full, anywhere], [full_shape, matrix_type],
-        [pltpu.VMEM((2,) + matrix_shape, weights.dtype), pltpu.SemaphoreType.DMA((6 * parts,))],
+        local_body, [full, in_vmem, in_vmem], [full, anywhere], [full_shape, matrix_type],
+        [pltpu.VMEM((2,) + matrix_shape, weights.dtype), pltpu.SemaphoreType.DMA((2 * parts,))],
         cost(columns, 2, 8 * columns * coeffs + 4 * matrix_bytes),
     )(bits, vectors, own_early, other_early)
     sent, late_other = lax.optimization_barrier((current, late_other))
@@ -211,7 +216,7 @@
         mine, code = call(
             core_body, [row_spec(c), row_spec(c), matrix_spec], [row_spec(0), code_spec],
             [chunk_shape, code_shape], [], cost(rows, 1, 14 * rows * coeffs + matrix_bytes),
-        )(bits, current, partner, matrix)
+        )(bits, in_hbm(current), in_hbm(partner), matrix)
         owns.append(mine)
         codes.append(code)
     arrived, later = [], []

time: 224 us -> 221 us (0.987)
  local copies, waits for them, and re-layouts: 18.7 us -> 10.8 us
  Pallas kernels: 29.8 us -> 33.5 us
    unnamed x32 -> x10, local copies, waits for them, and re-layouts: 13.7 us -> 5.76 us
    pallas_call x4, Pallas kernels: 6.62 us -> 11.5 us  [on_device(): call(core_body, [row_spec(c), row_spec(c), matrix_spec], [row_spec(0), co...]
  transfers between devices with their start and end apart: 14 -> 14, of which waited for: 7 -> 7; matrix products, arithmetic and copies ran while one was open for 1% -> 1% of each run, Pallas kernels for 12% -> 13%
where the time goes in v5:
time: 221 us; the launch traced here: 218 us
  waiting for transfers between devices  107 us (48%)
  starting transfers between devices  52.8 us (24%)
  Pallas kernels  33.5 us (15%)
  between operations  13.6 us (6%)
  local copies, waits for them, and re-layouts  10.8 us (5%)
    ppermute x11, waiting for transfers between devices, swapped(): lax.ppermute(shard, axis, [(i, i ^ 1 << apart) for i in range(lax.axis_si...  70 us
    ppermute x11, starting transfers between devices, swapped(): lax.ppermute(shard, axis, [(i, i ^ 1 << apart) for i in range(lax.axis_si...  48.3 us
    all_gather x1, waiting for transfers between devices, on_device(): lax.all_gather(jnp.stack([late, late_other], 1).reshape(-1, *late.shape[1...  20.2 us
    all_to_all x1, waiting for transfers between devices, around(): lax.all_to_all(jnp.broadcast_to(shard[None], (parts,) + shard.shape), 'na...  17.2 us
    pallas_call x4, Pallas kernels, on_device(): call(core_body, [row_spec(c), row_spec(c), matrix_spec], [row_spec(0), co...  11.5 us
    pallas_call x4, Pallas kernels, on_device(): call(last_body, specs, row_spec(c), full_shape, [], cost(rows, 1, 10 * ro...  7.7 us
    pallas_call x4, Pallas kernels, middle(): call(middle_body, [row_spec(0), code_spec, matrix_spec], [row_spec(0), co...  6.62 us
    pallas_call x1, Pallas kernels, on_device(): call(local_body, [full, in_vmem, in_vmem], [full, anywhere], [full_shape,...  6.34 us
  transfers between devices with their start and end apart: 14, of which 7 were waited for; matrix products, arithmetic and copies ran while one was open for 1% of the time, Pallas kernels for 13%

profile of v5, /device:TPU:480, one launch (start us, length us, event | category | flops | bytes accessed | tf_op | source)
XLA Modules:
  0.0 218.1 jit_solution(6428200956550339074)
XLA Ops:
  6.5 1.8 slice.6
  8.3 6.3 %collective-permute-start = (bf16[3,4,32,512]{3,2,1,0:T(8,128)(2,1)}, bf16[3,4,32,512]{3,2,1,0:T(8,128)(2,1)S(1)}, u32[]{:S(2)}, u32[]{:S(2)}) collective-permute-start(bf16[3,4,32,512]{3,2,1,0:T(8,128)(2,1)} %slice.6), channel_id=1, source_target_pairs={{0,4},{4,0},{1,5},{5,1},{2,6},{6,2},{3,7},{7,3},{8,12},{12,8},{9,1... | collective-permute-start | bytes 1179656 | tf_op jit(solution)/shard_map/ppermute | solution.py:19
  14.7 34.1 %collective-permute-done = bf16[3,4,32,512]{3,2,1,0:T(8,128)(2,1)S(1)} collective-permute-done((bf16[3,4,32,512]{3,2,1,0:T(8,128)(2,1)}, bf16[3,4,32,512]{3,2,1,0:T(8,128)(2,1)S(1)}, u32[]{:S(2)}, u32[]{:S(2)}) %collective-permute-start) | collective-permute-done | bytes 393248 | tf_op jit(solution)/shard_map/ppermute | solution.py:19
  50.1 4.5 %all-to-all-start = ((bf16[4,3,4,32,512]{4,3,2,1,0:T(8,128)(2,1)}), bf16[4,3,4,32,512]{4,3,2,1,0:T(8,128)(2,1)S(1)}, u32[]{:S(2)}, u32[]{:S(2)}) async-start(bf16[4,3,4,32,512]{4,3,2,1,0:T(8,128)(2,1)} %broadcast_in_dim.2), calls=%async_computation | async-start | bytes 3145728 | tf_op jit(solution)/shard_map/all_to_all | solution.py:160
  55.5 2.3 %collective-permute-start.1 = (bf16[2,4,32,512]{3,2,1,0:T(8,128)(2,1)S(1)}, bf16[2,4,32,512]{3,2,1,0:T(8,128)(2,1)S(1)}, u32[]{:S(2)}, u32[]{:S(2)}) collective-permute-start(bf16[2,4,32,512]{3,2,1,0:T(8,128)(2,1)S(1)} %get-tuple-element.32), channel_id=1, source_target_pairs={{0,4},{4,0},{1,5},{5,1},{2,6},{6,2},{3,7},{7,3},{8,12},{12,8},{9,1... | collective-permute-start | bytes 786440 | tf_op jit(solution)/shard_map/ppermute | solution.py:19
  57.9 17.2 %all-to-all-done.other = bf16[4,3,4,32,512]{4,3,2,1,0:T(8,128)(2,1)S(1)} async-done(((bf16[4,3,4,32,512]{4,3,2,1,0:T(8,128)(2,1)}), bf16[4,3,4,32,512]{4,3,2,1,0:T(8,128)(2,1)S(1)}, u32[]{:S(2)}, u32[]{:S(2)}) %all-to-all-start) | async-done | bytes 1572896 | tf_op jit(solution)/shard_map/all_to_all | solution.py:160
  76.5 6.3 %shard_map.28 = (f32[512,1024]{1,0:T(8,128)}, bf16[4,256,512]{2,1,0:T(8,128)(2,1)S(1)}) custom-call(s32[5]{0:T(128)S(1)} %stack.32.bits_ref, f32[512,1024]{1,0:T(8,128)} %x_ref.1, bf16[4,3,4,32,512]{4,3,2,1,0:T(8,128)(2,1)S(1)} %bitcast.10, bf16[4,3,4,32,512]{4,3,2,1,0:T(8,128)(2,1)S(1)} %all-to-all-done.other), custom_call_target="tpu_custom_call" | custom-call | tf_op jit(solution)/shard_map/pallas_call | solution.py:206
  82.9 3.2 %collective-permute-done.1 = bf16[2,4,32,512]{3,2,1,0:T(8,128)(2,1)S(1)} collective-permute-done((bf16[2,4,32,512]{3,2,1,0:T(8,128)(2,1)S(1)}, bf16[2,4,32,512]{3,2,1,0:T(8,128)(2,1)S(1)}, u32[]{:S(2)}, u32[]{:S(2)}) %collective-permute-start.1) | collective-permute-done | bytes 262176 | tf_op jit(solution)/shard_map/ppermute | solution.py:19
  86.1 1.9 collective-permute-start.2
  88.0 4.3 %collective-permute-done.2.partner_ref = f32[512,1024]{1,0:T(8,128)S(1)} collective-permute-done((f32[512,1024]{1,0:T(8,128)}, f32[512,1024]{1,0:T(8,128)S(1)}, u32[]{:S(2)}, u32[]{:S(2)}) %collective-permute-start.2) | collective-permute-done | bytes 2097184 | tf_op jit(solution)/shard_map/ppermute | solution.py:19
  93.7 3.2 %shard_map.30 = (f32[128,1024]{1,0:T(8,128)S(1)}, bf16[1040,128]{1,0:T(8,128)(2,1)}) custom-call(s32[5]{0:T(128)S(1)} %stack.32.bits_ref, f32[512,1024]{1,0:T(8,128)} %get-tuple-element.33.mine_ref, f32[512,1024]{1,0:T(8,128)} %copy-done.4, bf16[4,256,512]{2,1,0:T(8,128)(2,1)S(1)} %get-tuple-element.34.matrix), custom_call_target="tpu_custom_call" | custom-call | tf_op jit(solution)/shard_map/pallas_call | solution.py:216
  97.8 7.5 %collective-permute-start.7 = (bf16[1040,128]{1,0:T(8,128)(2,1)}, bf16[1040,128]{1,0:T(8,128)(2,1)}, u32[]{:S(2)}, u32[]{:S(2)}) collective-permute-start(bf16[1040,128]{1,0:T(8,128)(2,1)} %get-tuple-element.38), channel_id=1, source_target_pairs={{0,64},{8,72},{16,80},{24,88},{32,96},{40,104},{48,112},{56,120},{... | collective-permute-start | bytes 798728 | tf_op jit(solution)/shard_map/ppermute | solution.py:19
  105.4 3.2 %shard_map.36 = (f32[128,1024]{1,0:T(8,128)S(1)}, bf16[1040,128]{1,0:T(8,128)(2,1)}) custom-call(s32[5]{0:T(128)S(1)} %stack.32.bits_ref, f32[512,1024]{1,0:T(8,128)} %get-tuple-element.33.mine_ref, f32[512,1024]{1,0:T(8,128)} %copy-done.4, bf16[4,256,512]{2,1,0:T(8,128)(2,1)S(1)} %get-tuple-element.34.matrix), custom_call_target="tpu_custom_call" | custom-call | tf_op jit(solution)/shard_map/pallas_call | solution.py:216
  108.6 2.2 %collective-permute-start.9 = (bf16[1040,128]{1,0:T(8,128)(2,1)}, bf16[1040,128]{1,0:T(8,128)(2,1)S(1)}, u32[]{:S(2)}, u32[]{:S(2)}) collective-permute-start(bf16[1040,128]{1,0:T(8,128)(2,1)} %get-tuple-element.54), channel_id=1, source_target_pairs={{0,64},{8,72},{16,80},{24,88},{32,96},{40,104},{48,112},{56,120},{... | collective-permute-start | bytes 798728 | tf_op jit(solution)/shard_map/ppermute | solution.py:19
  110.8 2.5 %shard_map.33 = (f32[128,1024]{1,0:T(8,128)S(1)}, bf16[1040,128]{1,0:T(8,128)(2,1)S(1)}) custom-call(s32[5]{0:T(128)S(1)} %stack.32.bits_ref, f32[512,1024]{1,0:T(8,128)} %get-tuple-element.33.mine_ref, f32[512,1024]{1,0:T(8,128)} %copy-done.4, bf16[4,256,512]{2,1,0:T(8,128)(2,1)S(1)} %get-tuple-element.34.matrix), custom_call_target="tpu_custom_call" | custom-call | tf_op jit(solution)/shard_map/pallas_call | solution.py:216
  114.0 2.6 %shard_map.29 = (f32[128,1024]{1,0:T(8,128)S(1)}, bf16[1040,128]{1,0:T(8,128)(2,1)S(1)}) custom-call(s32[5]{0:T(128)S(1)} %stack.32.bits_ref, f32[512,1024]{1,0:T(8,128)} %get-tuple-element.33.mine_ref, f32[512,1024]{1,0:T(8,128)} %copy-done.4, bf16[4,256,512]{2,1,0:T(8,128)(2,1)S(1)} %get-tuple-element.34.matrix), custom_call_target="tpu_custom_call" | custom-call | tf_op jit(solution)/shard_map/pallas_call | solution.py:216
  117.3 20.2 %all-gather.4.cloned.1.call-done.gathered = bf16[4,4,4,32,512]{4,3,2,1,0:T(8,128)(2,1)} async-done(((bf16[1,4,4,32,512]{4,3,2,1,0:T(8,128)(2,1)}), bf16[4,4,4,32,512]{4,3,2,1,0:T(8,128)(2,1)}) %all-gather.4.cloned.1.call-update) | async-done | bytes 2097168 | tf_op jit(solution)/shard_map/all_gather | solution.py:232
  137.4 6.9 %collective-permute-start.5 = (bf16[1040,128]{1,0:T(8,128)(2,1)}, bf16[1040,128]{1,0:T(8,128)(2,1)S(1)}, u32[]{:S(2)}, u32[]{:S(2)}) collective-permute-start(bf16[1040,128]{1,0:T(8,128)(2,1)} %copy-done.3), channel_id=1, source_target_pairs={{0,64},{8,72},{16,80},{24,88},{32,96},{40,104},{48,112},{56,120},{... | collective-permute-start | bytes 798728 | tf_op jit(solution)/shard_map/ppermute | solution.py:19
  144.3 2.8 %collective-permute-start.3 = (bf16[1040,128]{1,0:T(8,128)(2,1)}, bf16[1040,128]{1,0:T(8,128)(2,1)S(1)}, u32[]{:S(2)}, u32[]{:S(2)}) collective-permute-start(bf16[1040,128]{1,0:T(8,128)(2,1)} %copy-done.2), channel_id=1, source_target_pairs={{0,64},{8,72},{16,80},{24,88},{32,96},{40,104},{48,112},{56,120},{... | collective-permute-start | bytes 798728 | tf_op jit(solution)/shard_map/ppermute | solution.py:19
  147.2 1.6 copy-done
  150.2 2.4 %shard_map.35 = (f32[128,1024]{1,0:T(8,128)S(1)}, bf16[1040,128]{1,0:T(8,128)(2,1)S(1)}) custom-call(s32[5]{0:T(128)S(1)} %stack.32.bits_ref, f32[128,1024]{1,0:T(8,128)S(1)} %get-tuple-element.50.mine_ref, bf16[1040,128]{1,0:T(8,128)(2,1)} %collective-permute-done.7.partner_ref, bf16[4,256,512]{2,1,0:T(8,128)(2,1)S(1)} %get-tuple-element.41.matrix), custom_call_target="tpu_custom_call" | custom-call | tf_op jit(solution)/shard_map/pallas_call | solution.py:225
  152.6 4.9 %collective-permute-start.8 = (bf16[1040,128]{1,0:T(8,128)(2,1)S(1)}, bf16[1040,128]{1,0:T(8,128)(2,1)S(1)}, u32[]{:S(2)}, u32[]{:S(2)}) collective-permute-start(bf16[1040,128]{1,0:T(8,128)(2,1)S(1)} %get-tuple-element.52), channel_id=1, source_target_pairs={{0,256},{8,264},{16,272},{24,280},{32,288},{40,296},{48,304},{56,3... | collective-permute-start | bytes 798728 | tf_op jit(solution)/shard_map/ppermute | solution.py:19
  157.5 27.0 %collective-permute-done.9.partner_ref = bf16[1040,128]{1,0:T(8,128)(2,1)S(1)} collective-permute-done((bf16[1040,128]{1,0:T(8,128)(2,1)}, bf16[1040,128]{1,0:T(8,128)(2,1)S(1)}, u32[]{:S(2)}, u32[]{:S(2)}) %collective-permute-start.9) | collective-permute-done | bytes 266272 | tf_op jit(solution)/shard_map/ppermute | solution.py:19
  184.5 1.4 shard_map.37
  185.9 4.9 %collective-permute-start.10 = (bf16[1040,128]{1,0:T(8,128)(2,1)S(1)}, bf16[1040,128]{1,0:T(8,128)(2,1)S(1)}, u32[]{:S(2)}, u32[]{:S(2)}) collective-permute-start(bf16[1040,128]{1,0:T(8,128)(2,1)S(1)} %get-tuple-element.56), channel_id=1, source_target_pairs={{0,256},{8,264},{16,272},{24,280},{32,288},{40,296},{48,304},{56,3... | collective-permute-start | bytes 798728 | tf_op jit(solution)/shard_map/ppermute | solution.py:19
  192.3 4.3 %collective-permute-start.6 = (bf16[1040,128]{1,0:T(8,128)(2,1)S(1)}, bf16[1040,128]{1,0:T(8,128)(2,1)S(1)}, u32[]{:S(2)}, u32[]{:S(2)}) collective-permute-start(bf16[1040,128]{1,0:T(8,128)(2,1)S(1)} %get-tuple-element.49), channel_id=1, source_target_pairs={{0,256},{8,264},{16,272},{24,280},{32,288},{40,296},{48,304},{56,3... | collective-permute-start | bytes 798728 | tf_op jit(solution)/shard_map/ppermute | solution.py:19
  196.6 1.4 shard_map.32
  198.0 4.2 %collective-permute-start.4 = (bf16[1040,128]{1,0:T(8,128)(2,1)S(1)}, bf16[1040,128]{1,0:T(8,128)(2,1)S(1)}, u32[]{:S(2)}, u32[]{:S(2)}) collective-permute-start(bf16[1040,128]{1,0:T(8,128)(2,1)S(1)} %get-tuple-element.43), channel_id=1, source_target_pairs={{0,256},{8,264},{16,272},{24,280},{32,288},{40,296},{48,304},{56,3... | collective-permute-start | bytes 798728 | tf_op jit(solution)/shard_map/ppermute | solution.py:19
  202.2 1.9 shard_map.38.rest_0_
  204.1 1.9 shard_map.39.rest_0_
  206.0 1.9 shard_map.40.rest_0_
  209.3 1.9 shard_map.41
  (28 shorter events, 11.7 us)
Async XLA Ops:
  6.5 68.6 %all-gather.6.cloned.1.call-start = ((), (), s32[]{:S(2)}) async-start(), calls=%async_computation.2 | async-start | bytes 1966080 | tf_op jit(solution)/shard_map/all_gather | solution.py:163
  8.3 40.4 %collective-permute-start = (bf16[3,4,32,512]{3,2,1,0:T(8,128)(2,1)}, bf16[3,4,32,512]{3,2,1,0:T(8,128)(2,1)S(1)}, u32[]{:S(2)}, u32[]{:S(2)}) collective-permute-start(bf16[3,4,32,512]{3,2,1,0:T(8,128)(2,1)} %slice.6), channel_id=1, source_target_pairs={{0,4},{4,0},{1,5},{5,1},{2,6},{6,2},{3,7},{7,3},{8,12},{12,8},{9,1... | collective-permute-start | bytes 1179656 | tf_op jit(solution)/shard_map/ppermute | solution.py:19
  50.1 25.1 %all-to-all-start = ((bf16[4,3,4,32,512]{4,3,2,1,0:T(8,128)(2,1)}), bf16[4,3,4,32,512]{4,3,2,1,0:T(8,128)(2,1)S(1)}, u32[]{:S(2)}, u32[]{:S(2)}) async-start(bf16[4,3,4,32,512]{4,3,2,1,0:T(8,128)(2,1)} %broadcast_in_dim.2), calls=%async_computation | async-start | bytes 3145728 | tf_op jit(solution)/shard_map/all_to_all | solution.py:160
  54.5 82.9 %all-gather.4.cloned.1.call-start = ((), (), s32[]{:S(2)}) async-start(), calls=%async_computation.1 | async-start | bytes 2621440 | tf_op jit(solution)/shard_map/all_gather | solution.py:232
  55.5 30.5 %collective-permute-start.1 = (bf16[2,4,32,512]{3,2,1,0:T(8,128)(2,1)S(1)}, bf16[2,4,32,512]{3,2,1,0:T(8,128)(2,1)S(1)}, u32[]{:S(2)}, u32[]{:S(2)}) collective-permute-start(bf16[2,4,32,512]{3,2,1,0:T(8,128)(2,1)S(1)} %get-tuple-element.32), channel_id=1, source_target_pairs={{0,4},{4,0},{1,5},{5,1},{2,6},{6,2},{3,7},{7,3},{8,12},{12,8},{9,1... | collective-permute-start | bytes 786440 | tf_op jit(solution)/shard_map/ppermute | solution.py:19
  75.1 1.4 copy-start.1
  86.1 6.3 %collective-permute-start.2 = (f32[512,1024]{1,0:T(8,128)}, f32[512,1024]{1,0:T(8,128)S(1)}, u32[]{:S(2)}, u32[]{:S(2)}) collective-permute-start(f32[512,1024]{1,0:T(8,128)} %get-tuple-element.33.mine_ref), channel_id=1, source_target_pairs={{0,8},{8,0},{16,24},{24,16},{32,40},{40,32},{48,56},{56,48},{64,72... | collective-permute-start | bytes 6291464 | tf_op jit(solution)/shard_map/ppermute | solution.py:19
  92.3 1.4 copy-start.4
  97.8 52.4 %collective-permute-start.7 = (bf16[1040,128]{1,0:T(8,128)(2,1)}, bf16[1040,128]{1,0:T(8,128)(2,1)}, u32[]{:S(2)}, u32[]{:S(2)}) collective-permute-start(bf16[1040,128]{1,0:T(8,128)(2,1)} %get-tuple-element.38), channel_id=1, source_target_pairs={{0,64},{8,72},{16,80},{24,88},{32,96},{40,104},{48,112},{56,120},{... | collective-permute-start | bytes 798728 | tf_op jit(solution)/shard_map/ppermute | solution.py:19
  108.6 75.9 %collective-permute-start.9 = (bf16[1040,128]{1,0:T(8,128)(2,1)}, bf16[1040,128]{1,0:T(8,128)(2,1)S(1)}, u32[]{:S(2)}, u32[]{:S(2)}) collective-permute-start(bf16[1040,128]{1,0:T(8,128)(2,1)} %get-tuple-element.54), channel_id=1, source_target_pairs={{0,64},{8,72},{16,80},{24,88},{32,96},{40,104},{48,112},{56,120},{... | collective-permute-start | bytes 798728 | tf_op jit(solution)/shard_map/ppermute | solution.py:19
  113.3 0.7 copy-start.3
  116.6 0.7 copy-start.2
  137.4 53.4 %collective-permute-start.5 = (bf16[1040,128]{1,0:T(8,128)(2,1)}, bf16[1040,128]{1,0:T(8,128)(2,1)S(1)}, u32[]{:S(2)}, u32[]{:S(2)}) collective-permute-start(bf16[1040,128]{1,0:T(8,128)(2,1)} %copy-done.3), channel_id=1, source_target_pairs={{0,64},{8,72},{16,80},{24,88},{32,96},{40,104},{48,112},{56,120},{... | collective-permute-start | bytes 798728 | tf_op jit(solution)/shard_map/ppermute | solution.py:19
  144.3 52.2 %collective-permute-start.3 = (bf16[1040,128]{1,0:T(8,128)(2,1)}, bf16[1040,128]{1,0:T(8,128)(2,1)S(1)}, u32[]{:S(2)}, u32[]{:S(2)}) collective-permute-start(bf16[1040,128]{1,0:T(8,128)(2,1)} %copy-done.2), channel_id=1, source_target_pairs={{0,64},{8,72},{16,80},{24,88},{32,96},{40,104},{48,112},{56,120},{... | collective-permute-start | bytes 798728 | tf_op jit(solution)/shard_map/ppermute | solution.py:19
  147.2 1.6 copy-start
  152.6 51.6 %collective-permute-start.8 = (bf16[1040,128]{1,0:T(8,128)(2,1)S(1)}, bf16[1040,128]{1,0:T(8,128)(2,1)S(1)}, u32[]{:S(2)}, u32[]{:S(2)}) collective-permute-start(bf16[1040,128]{1,0:T(8,128)(2,1)S(1)} %get-tuple-element.52), channel_id=1, source_target_pairs={{0,256},{8,264},{16,272},{24,280},{32,288},{40,296},{48,304},{56,3... | collective-permute-start | bytes 798728 | tf_op jit(solution)/shard_map/ppermute | solution.py:19
  185.9 16.3 %collective-permute-start.10 = (bf16[1040,128]{1,0:T(8,128)(2,1)S(1)}, bf16[1040,128]{1,0:T(8,128)(2,1)S(1)}, u32[]{:S(2)}, u32[]{:S(2)}) collective-permute-start(bf16[1040,128]{1,0:T(8,128)(2,1)S(1)} %get-tuple-element.56), channel_id=1, source_target_pairs={{0,256},{8,264},{16,272},{24,280},{32,288},{40,296},{48,304},{56,3... | collective-permute-start | bytes 798728 | tf_op jit(solution)/shard_map/ppermute | solution.py:19
  192.3 13.8 %collective-permute-start.6 = (bf16[1040,128]{1,0:T(8,128)(2,1)S(1)}, bf16[1040,128]{1,0:T(8,128)(2,1)S(1)}, u32[]{:S(2)}, u32[]{:S(2)}) collective-permute-start(bf16[1040,128]{1,0:T(8,128)(2,1)S(1)} %get-tuple-element.49), channel_id=1, source_target_pairs={{0,256},{8,264},{16,272},{24,280},{32,288},{40,296},{48,304},{56,3... | collective-permute-start | bytes 798728 | tf_op jit(solution)/shard_map/ppermute | solution.py:19
  198.0 11.4 %collective-permute-start.4 = (bf16[1040,128]{1,0:T(8,128)(2,1)S(1)}, bf16[1040,128]{1,0:T(8,128)(2,1)S(1)}, u32[]{:S(2)}, u32[]{:S(2)}) collective-permute-start(bf16[1040,128]{1,0:T(8,128)(2,1)S(1)} %get-tuple-element.43), channel_id=1, source_target_pairs={{0,256},{8,264},{16,272},{24,280},{32,288},{40,296},{48,304},{56,3... | collective-permute-start | bytes 798728 | tf_op jit(solution)/shard_map/ppermute | solution.py:19
Sparse Core Ops, SparseCore 0:
  9.5 33.2 all-gather.5
  97.9 39.4 all-gather.3
